TPU v7x, 512 devices: a whole 4x4x16 slice. The times are simulated.
512 devices in a mesh: span: 64 (over z, x), width: 8 (over y, core).
Axes of the slice: x: 4, y: 4, z: 16, core: 2. Of those that a mesh axis runs over, the one named last changes fastest.
Arguments:
- right_side: float32 [32, 512, 4096], P(None, 'span', 'width'), may hold values from -6 to 6
- diffusivity: float32 [32, 512, 4096], P(None, 'span', 'width'), may hold values from 0.2 to 5
- reaction: float32 [32, 512, 4096], P(None, 'span', 'width'), may hold values from 0.01 to 0.2
Outputs:
- correction: float32 [32, 512, 4096], P(None, 'span', 'width')
All inputs are finite; a program needn't handle non-finite values.
Results may differ from a plain program's by a relative error of at most 0.0003.
Values sent between devices are 32-bit elements; how exact they have to be, the bound alone decides.
A program may use at most 128 MiB of HBM per device.

v0:
```python
import jax
import jax.numpy as jnp
from jax import lax
from jax.sharding import PartitionSpec as P

LEVELS = 6
COARSE_SWEEPS = 3


relax_weight = 0.8


def with_halo(cells, sides, width):
    for axis, dim in sides:
        count = lax.axis_size(axis)
        ends = count - 1
        head = lax.slice_in_dim(cells, 0, width, axis=dim)
        tail = lax.slice_in_dim(cells, cells.shape[dim] - width, cells.shape[dim], axis=dim)
        cells = jnp.concatenate(
            [
                lax.ppermute(tail, axis, [(i, (i + 1) % count) for i in range(ends)]),
                cells,
                lax.ppermute(head, axis, [((i + 1) % count, i) for i in range(ends)]),
            ],
            axis=dim,
        )
    return cells


def from_behind(value, axis, steps):
    count = lax.axis_size(axis)
    initial, last = (max(0, -steps), min(count, count - steps))
    return lax.ppermute(value, axis, [(source, source + steps) for source in range(initial, last)])


def partner_2(block, axis, distance):
    count = lax.axis_size(axis)
    route = []
    for low in range(count):
        high = low | 1 << distance
        if high != low and high < count:
            route += [(low, high), (high, low)]
    return lax.ppermute(block, axis, route)


def harmonic(first, second):
    return 2.0 * first * second / (first + second)


def level_group(cells_x, grid_level):
    return max(1, 4 * 2**grid_level // cells_x)


def layout(cells_x, grid_level, span_count):
    group_size = level_group(cells_x, grid_level)
    span_whole = group_size >= span_count
    return (group_size, span_whole, False)


def extend(field, grid_level, cells_x, span_count):
    group_size, span_whole, width_whole = layout(cells_x, grid_level, span_count)
    if group_size == 1 and (not span_whole) and (not width_whole):
        return with_halo(field, (("span", 1), ("width", 2)), 1)
    widened = with_halo(field, (("width", 2),), 1)
    below_plane = from_behind(widened[:, -1:, :], "span", group_size)
    above_plane = from_behind(widened[:, :1, :], "span", -group_size)
    return jnp.concatenate([below_plane, widened, above_plane], axis=1)


def face_terms(conduct, binding, grid_level, cells_x, span_count):
    padded = extend(conduct, grid_level, cells_x, span_count)
    depth_pad = jnp.pad(conduct, ((1, 1), (0, 0), (0, 0)))
    face_scale = 0.25**grid_level
    west = face_scale * harmonic(conduct, padded[:, :-2, 1:-1])
    east = face_scale * harmonic(conduct, padded[:, 2:, 1:-1])
    south = face_scale * harmonic(conduct, padded[:, 1:-1, :-2])
    north = face_scale * harmonic(conduct, padded[:, 1:-1, 2:])
    upward = face_scale * harmonic(conduct, depth_pad[:-2])
    downward = face_scale * harmonic(conduct, depth_pad[2:])
    diagonal = west + east + south + north + upward + downward + face_scale * binding
    return (west, east, south, north, upward, downward, diagonal)


def operate(field, coeffs, grid_level, cells_x, span_count):
    padded = extend(field, grid_level, cells_x, span_count)
    depth_pad = jnp.pad(field, ((1, 1), (0, 0), (0, 0)))
    beside = coeffs[0] * padded[:, :-2, 1:-1] + coeffs[1] * padded[:, 2:, 1:-1]
    beside = beside + coeffs[2] * padded[:, 1:-1, :-2] + coeffs[3] * padded[:, 1:-1, 2:]
    beside = beside + coeffs[4] * depth_pad[:-2] + coeffs[5] * depth_pad[2:]
    return coeffs[6] * field - beside


def restrict(field):
    depth, first, second = field.shape
    return jnp.mean(field.reshape(depth, first // 2, 2, second // 2, 2), axis=(2, 4))


def pair_up(fields, group_size):
    bit_index = group_size.bit_length() - 1
    stacked = jnp.stack(fields)
    partner = partner_2(stacked, "span", bit_index)
    upper_half = lax.axis_index("span") // group_size % 2 == 1
    joined = jnp.where(
        upper_half,
        jnp.concatenate([partner, stacked], axis=2),
        jnp.concatenate([stacked, partner], axis=2),
    )
    return tuple((joined[position] for position in range(len(fields))))


def descend(fields, grid_level, cells_x):
    coarse = tuple((restrict(field) for field in fields))
    group_now = level_group(cells_x, grid_level)
    group_next = level_group(cells_x, grid_level + 1)
    if group_next > group_now:
        coarse = pair_up(coarse, group_now)
    return tuple(coarse)


def prolong(coarse, fine_shape, grid_level, cells_x, span_count):
    group_fine, whole_fine, width_fine = layout(cells_x, grid_level, span_count)
    group_coarse, whole_coarse, width_coarse = layout(cells_x, grid_level + 1, span_count)
    depth, extent_x, extent_y = fine_shape
    span_at = lax.axis_index("span")
    offset_x = span_at // group_fine * (extent_x // 2) - span_at // group_coarse * coarse.shape[1]
    offset_y = jnp.zeros((), jnp.int32)
    coarse_part = lax.dynamic_slice(
        coarse,
        (jnp.zeros((), jnp.int32), offset_x, offset_y),
        (depth, extent_x // 2, extent_y // 2),
    )
    return jnp.repeat(jnp.repeat(coarse_part, 2, axis=1), 2, axis=2)


def on_device(right_side, diffusivity, reaction):
    cells_x = diffusivity.shape[1]
    span_count = lax.axis_size("span")
    conduct = diffusivity
    binding = reaction
    all_coeffs = []
    for grid_level in range(LEVELS):
        all_coeffs.append(face_terms(conduct, binding, grid_level, cells_x, span_count))
        if grid_level < LEVELS - 1:
            conduct, binding = descend((conduct, binding), grid_level, cells_x)
    source = right_side
    saved = []
    for grid_level in range(LEVELS - 1):
        coeffs = all_coeffs[grid_level]
        smooth_one = relax_weight * source / coeffs[6]
        defect = source - operate(smooth_one, coeffs, grid_level, cells_x, span_count)
        saved.append((source, smooth_one))
        source = descend((defect,), grid_level, cells_x)[0]
    coeffs = all_coeffs[LEVELS - 1]
    iterate = relax_weight * source / coeffs[6]
    for sweep_index in range(COARSE_SWEEPS - 1):
        iterate = (
            iterate
            + relax_weight
            * (source - operate(iterate, coeffs, LEVELS - 1, cells_x, span_count))
            / coeffs[6]
        )
    for grid_level in range(LEVELS - 2, -1, -1):
        source, smooth_one = saved[grid_level]
        coeffs = all_coeffs[grid_level]
        lifted = smooth_one + prolong(iterate, smooth_one.shape, grid_level, cells_x, span_count)
        iterate = (
            lifted
            + relax_weight
            * (source - operate(lifted, coeffs, grid_level, cells_x, span_count))
            / coeffs[6]
        )
    return iterate


def solution(mesh):
    in_specs = (P(None, "span", "width"), P(None, "span", "width"), P(None, "span", "width"))
    out_specs = P(None, "span", "width")
    return jax.shard_map(
        on_device, mesh=mesh, in_specs=in_specs, out_specs=out_specs, check_vma=False
    )
```

profile of v0, /device:TPU:15, one launch (start us, length us, event | category | flops | bytes accessed | tf_op | source)
XLA Modules:
  0.0 501.9 jit_solution(12904393720993874857)
XLA Ops:
  11.6 5.5 %collective-permute-start.8 = (f32[32,1,256]{2,0,1:T(8,128)}, f32[32,1,256]{2,0,1:T(8,128)}, u32[]{:S(2)}, u32[]{:S(2)}) collective-permute-start(f32[32,1,256]{2,0,1:T(8,128)} %get-tuple-element.90), channel_id=1, source_target_pairs={{0,8},{8,16},{16,24},{24,32},{32,40},{40,48},{48,56},{56,64},{64,7... | collective-permute-start | bytes 98312 | tf_op jit(solution)/shard_map/ppermute | solution.py:21
  19.8 4.6 collective-permute-start.2
  36.3 5.8 %collective-permute-start.4 = (f32[32,1,512]{2,1,0:T(1,128)S(1)}, f32[32,1,512]{2,1,0:T(1,128)S(1)}, u32[]{:S(2)}, u32[]{:S(2)}) collective-permute-start(f32[32,1,512]{2,1,0:T(1,128)S(1)} %get-tuple-element.40), channel_id=1, source_target_pairs={{0,8},{8,16},{16,24},{24,32},{32,40},{40,48},{48,56},{56,64},{64,7... | collective-permute-start | bytes 196616 | tf_op jit(solution)/shard_map/ppermute | solution.py:21
  45.2 4.9 collective-permute-done.5
  50.1 5.1 %collective-permute-start.6 = (f32[32,10,1]{2,0,1:T(8,128)S(1)}, f32[32,10,1]{2,0,1:T(8,128)S(1)}, u32[]{:S(2)}, u32[]{:S(2)}) collective-permute-start(f32[32,10,1]{2,0,1:T(8,128)S(1)} %get-tuple-element.32), channel_id=1, source_target_pairs={{0,1},{1,2},{2,3},{3,4},{4,5},{5,6},{6,7},{8,9},{9,10},{10,11},{11... | collective-permute-start | bytes 3848 | tf_op jit(solution)/shard_map/ppermute | solution.py:21
  135.8 5.1 %collective-permute-start.22 = (f32[32,4,1]{2,0,1:T(8,128)S(1)}, f32[32,4,1]{2,0,1:T(8,128)S(1)}, u32[]{:S(2)}, u32[]{:S(2)}) collective-permute-start(f32[32,4,1]{2,0,1:T(8,128)S(1)} %get-tuple-element.108), channel_id=1, source_target_pairs={{0,1},{1,2},{2,3},{3,4},{4,5},{5,6},{6,7},{8,9},{9,10},{10,11},{11... | collective-permute-start | bytes 1544 | tf_op jit(solution)/shard_map/ppermute | solution.py:21
  147.1 5.4 %collective-permute-start.24 = (f32[32,1,130]{2,0,1:T(8,128)}, f32[32,1,130]{2,0,1:T(8,128)}, u32[]{:S(2)}, u32[]{:S(2)}) collective-permute-start(f32[32,1,130]{2,0,1:T(8,128)} %get-tuple-element.61), channel_id=1, source_target_pairs={{0,16},{8,24},{16,32},{24,40},{32,48},{40,56},{48,64},{56,72},{64,... | collective-permute-start | bytes 49928 | tf_op jit(solution)/shard_map/ppermute | solution.py:33
  172.2 7.0 %collective-permute-start.37 = (f32[2,32,2,32]{1,3,2,0:T(8,128)}, f32[2,32,2,32]{1,3,2,0:T(8,128)}, u32[]{:S(2)}, u32[]{:S(2)}) collective-permute-start(f32[2,32,2,32]{1,3,2,0:T(8,128)} %pad_maximum_fusion.113), channel_id=1, source_target_pairs={{0,32},{32,0},{8,40},{40,8},{16,48},{48,16},{24,56},{56,24},{64,96... | collective-permute-start | bytes 49160 | tf_op jit(solution)/shard_map/ppermute | solution.py:43
  200.3 4.5 collective-permute-start.38
  220.9 12.9 %collective-permute-start.47 = (f32[2,32,2,16]{1,3,2,0:T(8,128)}, f32[2,32,2,16]{1,3,2,0:T(8,128)}, u32[]{:S(2)}, u32[]{:S(2)}) collective-permute-start(f32[2,32,2,16]{1,3,2,0:T(8,128)} %pad_maximum_fusion.147), channel_id=1, source_target_pairs={{0,64},{64,0},{8,72},{72,8},{16,80},{80,16},{24,88},{88,24},{32,96... | collective-permute-start | bytes 24584 | tf_op jit(solution)/shard_map/ppermute | solution.py:43
  243.4 4.9 collective-permute-start.40
  259.7 7.9 %collective-permute-start.36 = (f32[1,32,2,32]{1,3,2,0:T(8,128)S(1)}, f32[1,32,2,32]{1,3,2,0:T(8,128)S(1)}, u32[]{:S(2)}, u32[]{:S(2)}) collective-permute-start(f32[1,32,2,32]{1,3,2,0:T(8,128)S(1)} %get-tuple-element.125), channel_id=1, source_target_pairs={{0,32},{32,0},{8,40},{40,8},{16,48},{48,16},{24,56},{56,24},{64,96... | collective-permute-start | bytes 24584 | tf_op jit(solution)/shard_map/ppermute | solution.py:43
  269.9 5.4 %collective-permute-start.42 = (f32[32,4,1]{0,2,1:T(1,128)S(1)}, f32[32,4,1]{0,2,1:T(1,128)S(1)}, u32[]{:S(2)}, u32[]{:S(2)}) collective-permute-start(f32[32,4,1]{0,2,1:T(1,128)S(1)} %get-tuple-element.102), channel_id=1, source_target_pairs={{0,1},{1,2},{2,3},{3,4},{4,5},{5,6},{6,7},{8,9},{9,10},{10,11},{11... | collective-permute-start | bytes 1544 | tf_op jit(solution)/shard_map/ppermute | solution.py:21
  280.2 6.3 %collective-permute-start.44 = (f32[32,1,34]{0,2,1:T(8,128)S(1)}, f32[32,1,34]{0,2,1:T(8,128)S(1)}, u32[]{:S(2)}, u32[]{:S(2)}) collective-permute-start(f32[32,1,34]{0,2,1:T(8,128)S(1)} %get-tuple-element.94), channel_id=1, source_target_pairs={{0,64},{8,72},{16,80},{24,88},{32,96},{40,104},{48,112},{56,120},{... | collective-permute-start | bytes 13064 | tf_op jit(solution)/shard_map/ppermute | solution.py:33
  296.0 5.7 %collective-permute-start.46 = (f32[1,32,2,16]{1,3,2,0:T(8,128)S(1)}, f32[1,32,2,16]{1,3,2,0:T(8,128)S(1)}, u32[]{:S(2)}, u32[]{:S(2)}) collective-permute-start(f32[1,32,2,16]{1,3,2,0:T(8,128)S(1)} %get-tuple-element.129), channel_id=1, source_target_pairs={{0,64},{64,0},{8,72},{72,8},{16,80},{80,16},{24,88},{88,24},{32,96... | collective-permute-start | bytes 12296 | tf_op jit(solution)/shard_map/ppermute | solution.py:43
  302.5 5.3 %collective-permute-start.50 = (f32[32,1,18]{0,2,1:T(8,128)S(1)}, f32[32,1,18]{0,2,1:T(8,128)S(1)}, u32[]{:S(2)}, u32[]{:S(2)}) collective-permute-start(f32[32,1,18]{0,2,1:T(8,128)S(1)} %get-tuple-element.116), channel_id=1, source_target_pairs={{0,128},{8,136},{16,144},{24,152},{32,160},{40,168},{48,176},{56,1... | collective-permute-start | bytes 6920 | tf_op jit(solution)/shard_map/ppermute | solution.py:33
  309.1 7.0 %collective-permute-done.51 = f32[32,1,18]{0,2,1:T(8,128)S(1)} collective-permute-done((f32[32,1,18]{0,2,1:T(8,128)S(1)}, f32[32,1,18]{0,2,1:T(8,128)S(1)}, u32[]{:S(2)}, u32[]{:S(2)}) %collective-permute-start.51) | collective-permute-done | bytes 2336 | tf_op jit(solution)/shard_map/ppermute | solution.py:33
  317.9 5.1 %collective-permute-start.52 = (f32[32,4,1]{0,2,1:T(1,128)S(1)}, f32[32,4,1]{0,2,1:T(1,128)S(1)}, u32[]{:S(2)}, u32[]{:S(2)}) collective-permute-start(f32[32,4,1]{0,2,1:T(1,128)S(1)} %get-tuple-element.120), channel_id=1, source_target_pairs={{0,1},{1,2},{2,3},{3,4},{4,5},{5,6},{6,7},{8,9},{9,10},{10,11},{11... | collective-permute-start | bytes 1544 | tf_op jit(solution)/shard_map/ppermute | solution.py:21
  328.5 4.7 collective-permute-start.54
  334.5 7.3 %collective-permute-done.55 = f32[32,1,18]{0,2,1:T(8,128)} collective-permute-done((f32[32,1,18]{0,2,1:T(8,128)}, f32[32,1,18]{0,2,1:T(8,128)}, u32[]{:S(2)}, u32[]{:S(2)}) %collective-permute-start.55) | collective-permute-done | bytes 2336 | tf_op jit(solution)/shard_map/ppermute | solution.py:33
  357.4 6.1 %collective-permute-done.59 = f32[32,1,18]{0,2,1:T(8,128)S(1)} collective-permute-done((f32[32,1,18]{0,2,1:T(8,128)S(1)}, f32[32,1,18]{0,2,1:T(8,128)S(1)}, u32[]{:S(2)}, u32[]{:S(2)}) %collective-permute-start.59) | collective-permute-done | bytes 2336 | tf_op jit(solution)/shard_map/ppermute | solution.py:33
  447.4 4.7 collective-permute-start.72
  454.1 4.9 collective-permute-done.73
  459.0 4.8 collective-permute-start.74
  (384 shorter events, 359.3 us)
Async XLA Ops:
  1.9 17.3 %collective-permute-start = (f32[32,1,512]{2,1,0:T(1,128)}, f32[32,1,512]{2,1,0:T(1,128)S(1)}, u32[]{:S(2)}, u32[]{:S(2)}) collective-permute-start(f32[32,1,512]{2,1,0:T(1,128)} %get-tuple-element.43), channel_id=1, source_target_pairs={{0,8},{8,16},{16,24},{24,32},{32,40},{40,48},{48,56},{56,64},{64,7... | collective-permute-start | bytes 196616 | tf_op jit(solution)/shard_map/ppermute | solution.py:21
  5.4 14.2 %collective-permute-start.1 = (f32[32,1,512]{2,1,0:T(1,128)}, f32[32,1,512]{2,1,0:T(1,128)S(1)}, u32[]{:S(2)}, u32[]{:S(2)}) collective-permute-start(f32[32,1,512]{2,1,0:T(1,128)} %get-tuple-element.42), channel_id=1, source_target_pairs={{8,0},{16,8},{24,16},{32,24},{40,32},{48,40},{56,48},{64,56},{72,6... | collective-permute-start | bytes 196616 | tf_op jit(solution)/shard_map/ppermute | solution.py:23
  11.6 30.5 %collective-permute-start.8 = (f32[32,1,256]{2,0,1:T(8,128)}, f32[32,1,256]{2,0,1:T(8,128)}, u32[]{:S(2)}, u32[]{:S(2)}) collective-permute-start(f32[32,1,256]{2,0,1:T(8,128)} %get-tuple-element.90), channel_id=1, source_target_pairs={{0,8},{8,16},{16,24},{24,32},{32,40},{40,48},{48,56},{56,64},{64,7... | collective-permute-start | bytes 98312 | tf_op jit(solution)/shard_map/ppermute | solution.py:21
  17.1 25.0 %collective-permute-start.9 = (f32[32,1,256]{2,0,1:T(8,128)}, f32[32,1,256]{2,0,1:T(8,128)}, u32[]{:S(2)}, u32[]{:S(2)}) collective-permute-start(f32[32,1,256]{2,0,1:T(8,128)} %get-tuple-element.91), channel_id=1, source_target_pairs={{8,0},{16,8},{24,16},{32,24},{40,32},{48,40},{56,48},{64,56},{72,6... | collective-permute-start | bytes 98312 | tf_op jit(solution)/shard_map/ppermute | solution.py:23
  19.8 13.8 %collective-permute-start.2 = (f32[32,10,1]{2,0,1:T(8,128)S(1)}, f32[32,10,1]{2,0,1:T(8,128)}, u32[]{:S(2)}, u32[]{:S(2)}) collective-permute-start(f32[32,10,1]{2,0,1:T(8,128)S(1)} %get-tuple-element.37), channel_id=1, source_target_pairs={{0,1},{1,2},{2,3},{3,4},{4,5},{5,6},{6,7},{8,9},{9,10},{10,11},{11... | collective-permute-start | bytes 3848 | tf_op jit(solution)/shard_map/ppermute | solution.py:21
  50.1 13.5 %collective-permute-start.6 = (f32[32,10,1]{2,0,1:T(8,128)S(1)}, f32[32,10,1]{2,0,1:T(8,128)S(1)}, u32[]{:S(2)}, u32[]{:S(2)}) collective-permute-start(f32[32,10,1]{2,0,1:T(8,128)S(1)} %get-tuple-element.32), channel_id=1, source_target_pairs={{0,1},{1,2},{2,3},{3,4},{4,5},{5,6},{6,7},{8,9},{9,10},{10,11},{11... | collective-permute-start | bytes 3848 | tf_op jit(solution)/shard_map/ppermute | solution.py:21
  57.9 17.7 %collective-permute-start.10 = (f32[32,6,1]{2,0,1:T(8,128)}, f32[32,6,1]{2,0,1:T(8,128)S(1)}, u32[]{:S(2)}, u32[]{:S(2)}) collective-permute-start(f32[32,6,1]{2,0,1:T(8,128)} %get-tuple-element.72), channel_id=1, source_target_pairs={{0,1},{1,2},{2,3},{3,4},{4,5},{5,6},{6,7},{8,9},{9,10},{10,11},{11... | collective-permute-start | bytes 2312 | tf_op jit(solution)/shard_map/ppermute | solution.py:21
  61.5 14.7 %collective-permute-start.11 = (f32[32,6,1]{2,0,1:T(8,128)}, f32[32,6,1]{2,0,1:T(8,128)}, u32[]{:S(2)}, u32[]{:S(2)}) collective-permute-start(f32[32,6,1]{2,0,1:T(8,128)} %get-tuple-element.71), channel_id=1, source_target_pairs={{1,0},{2,1},{3,2},{4,3},{5,4},{6,5},{7,6},{9,8},{10,9},{11,10},{12... | collective-permute-start | bytes 2312 | tf_op jit(solution)/shard_map/ppermute | solution.py:23
  107.1 24.1 %collective-permute-start.16 = (f32[1,32,2,128]{3,1,2,0:T(8,128)}, f32[1,32,2,128]{3,1,2,0:T(8,128)}, u32[]{:S(2)}, u32[]{:S(2)}) collective-permute-start(f32[1,32,2,128]{3,1,2,0:T(8,128)} %get-tuple-element.127), channel_id=1, source_target_pairs={{0,8},{8,0},{16,24},{24,16},{32,40},{40,32},{48,56},{56,48},{64,72... | collective-permute-start | bytes 98312 | tf_op jit(solution)/shard_map/ppermute | solution.py:43
  147.1 38.8 %collective-permute-start.24 = (f32[32,1,130]{2,0,1:T(8,128)}, f32[32,1,130]{2,0,1:T(8,128)}, u32[]{:S(2)}, u32[]{:S(2)}) collective-permute-start(f32[32,1,130]{2,0,1:T(8,128)} %get-tuple-element.61), channel_id=1, source_target_pairs={{0,16},{8,24},{16,32},{24,40},{32,48},{40,56},{48,64},{56,72},{64,... | collective-permute-start | bytes 49928 | tf_op jit(solution)/shard_map/ppermute | solution.py:33
  152.5 33.4 %collective-permute-start.25 = (f32[32,1,130]{2,0,1:T(8,128)}, f32[32,1,130]{2,0,1:T(8,128)}, u32[]{:S(2)}, u32[]{:S(2)}) collective-permute-start(f32[32,1,130]{2,0,1:T(8,128)} %get-tuple-element.62), channel_id=1, source_target_pairs={{16,0},{24,8},{32,16},{40,24},{48,32},{56,40},{64,48},{72,56},{80,... | collective-permute-start | bytes 49928 | tf_op jit(solution)/shard_map/ppermute | solution.py:33
  156.8 22.3 %collective-permute-start.28 = (f32[32,4,1]{0,2,1:T(1,128)S(1)}, f32[32,4,1]{0,2,1:T(1,128)S(1)}, u32[]{:S(2)}, u32[]{:S(2)}) collective-permute-start(f32[32,4,1]{0,2,1:T(1,128)S(1)} %get-tuple-element.82), channel_id=1, source_target_pairs={{0,1},{1,2},{2,3},{3,4},{4,5},{5,6},{6,7},{8,9},{9,10},{10,11},{11... | collective-permute-start | bytes 1544 | tf_op jit(solution)/shard_map/ppermute | solution.py:21
  161.3 18.7 %collective-permute-start.29 = (f32[32,4,1]{0,2,1:T(1,128)S(1)}, f32[32,4,1]{0,2,1:T(1,128)S(1)}, u32[]{:S(2)}, u32[]{:S(2)}) collective-permute-start(f32[32,4,1]{0,2,1:T(1,128)S(1)} %get-tuple-element.83), channel_id=1, source_target_pairs={{1,0},{2,1},{3,2},{4,3},{5,4},{6,5},{7,6},{9,8},{10,9},{11,10},{12... | collective-permute-start | bytes 1544 | tf_op jit(solution)/shard_map/ppermute | solution.py:23
  172.2 25.2 %collective-permute-start.37 = (f32[2,32,2,32]{1,3,2,0:T(8,128)}, f32[2,32,2,32]{1,3,2,0:T(8,128)}, u32[]{:S(2)}, u32[]{:S(2)}) collective-permute-start(f32[2,32,2,32]{1,3,2,0:T(8,128)} %pad_maximum_fusion.113), channel_id=1, source_target_pairs={{0,32},{32,0},{8,40},{40,8},{16,48},{48,16},{24,56},{56,24},{64,96... | collective-permute-start | bytes 49160 | tf_op jit(solution)/shard_map/ppermute | solution.py:43
  191.4 19.8 %collective-permute-start.26 = (f32[1,32,2,64]{1,3,2,0:T(8,128)}, f32[1,32,2,64]{1,3,2,0:T(8,128)}, u32[]{:S(2)}, u32[]{:S(2)}) collective-permute-start(f32[1,32,2,64]{1,3,2,0:T(8,128)} %get-tuple-element.107), channel_id=1, source_target_pairs={{0,16},{16,0},{8,24},{24,8},{32,48},{48,32},{40,56},{56,40},{64,80... | collective-permute-start | bytes 49160 | tf_op jit(solution)/shard_map/ppermute | solution.py:43
  200.3 41.8 %collective-permute-start.38 = (f32[32,4,1]{0,2,1:T(1,128)}, f32[32,4,1]{0,2,1:T(1,128)}, u32[]{:S(2)}, u32[]{:S(2)}) collective-permute-start(f32[32,4,1]{0,2,1:T(1,128)} %get-tuple-element.104), channel_id=1, source_target_pairs={{0,1},{1,2},{2,3},{3,4},{4,5},{5,6},{6,7},{8,9},{9,10},{10,11},{11... | collective-permute-start | bytes 1544 | tf_op jit(solution)/shard_map/ppermute | solution.py:21
  204.8 37.3 %collective-permute-start.39 = (f32[32,4,1]{0,2,1:T(1,128)}, f32[32,4,1]{0,2,1:T(1,128)}, u32[]{:S(2)}, u32[]{:S(2)}) collective-permute-start(f32[32,4,1]{0,2,1:T(1,128)} %get-tuple-element.105), channel_id=1, source_target_pairs={{1,0},{2,1},{3,2},{4,3},{5,4},{6,5},{7,6},{9,8},{10,9},{11,10},{12... | collective-permute-start | bytes 1544 | tf_op jit(solution)/shard_map/ppermute | solution.py:23
  214.7 20.7 %collective-permute-start.32 = (f32[32,4,1]{0,2,1:T(1,128)}, f32[32,4,1]{0,2,1:T(1,128)}, u32[]{:S(2)}, u32[]{:S(2)}) collective-permute-start(f32[32,4,1]{0,2,1:T(1,128)} %get-tuple-element.80), channel_id=1, source_target_pairs={{0,1},{1,2},{2,3},{3,4},{4,5},{5,6},{6,7},{8,9},{9,10},{10,11},{11... | collective-permute-start | bytes 1544 | tf_op jit(solution)/shard_map/ppermute | solution.py:21
  218.4 18.5 %collective-permute-start.33 = (f32[32,4,1]{0,2,1:T(1,128)}, f32[32,4,1]{0,2,1:T(1,128)}, u32[]{:S(2)}, u32[]{:S(2)}) collective-permute-start(f32[32,4,1]{0,2,1:T(1,128)} %get-tuple-element.81), channel_id=1, source_target_pairs={{1,0},{2,1},{3,2},{4,3},{5,4},{6,5},{7,6},{9,8},{10,9},{11,10},{12... | collective-permute-start | bytes 1544 | tf_op jit(solution)/shard_map/ppermute | solution.py:23
  220.9 46.6 %collective-permute-start.47 = (f32[2,32,2,16]{1,3,2,0:T(8,128)}, f32[2,32,2,16]{1,3,2,0:T(8,128)}, u32[]{:S(2)}, u32[]{:S(2)}) collective-permute-start(f32[2,32,2,16]{1,3,2,0:T(8,128)} %pad_maximum_fusion.147), channel_id=1, source_target_pairs={{0,64},{64,0},{8,72},{72,8},{16,80},{80,16},{24,88},{88,24},{32,96... | collective-permute-start | bytes 24584 | tf_op jit(solution)/shard_map/ppermute | solution.py:43
  243.4 25.0 %collective-permute-start.40 = (f32[32,1,34]{0,2,1:T(8,128)}, f32[32,1,34]{0,2,1:T(8,128)}, u32[]{:S(2)}, u32[]{:S(2)}) collective-permute-start(f32[32,1,34]{0,2,1:T(8,128)} %get-tuple-element.96), channel_id=1, source_target_pairs={{0,64},{8,72},{16,80},{24,88},{32,96},{40,104},{48,112},{56,120},{... | collective-permute-start | bytes 13064 | tf_op jit(solution)/shard_map/ppermute | solution.py:33
  248.3 20.2 %collective-permute-start.41 = (f32[32,1,34]{0,2,1:T(8,128)}, f32[32,1,34]{0,2,1:T(8,128)}, u32[]{:S(2)}, u32[]{:S(2)}) collective-permute-start(f32[32,1,34]{0,2,1:T(8,128)} %get-tuple-element.97), channel_id=1, source_target_pairs={{64,0},{72,8},{80,16},{88,24},{96,32},{104,40},{112,48},{120,56},{... | collective-permute-start | bytes 13064 | tf_op jit(solution)/shard_map/ppermute | solution.py:33
  288.4 13.3 %collective-permute-start.48 = (f32[32,4,1]{0,2,1:T(1,128)}, f32[32,4,1]{0,2,1:T(1,128)}, u32[]{:S(2)}, u32[]{:S(2)}) collective-permute-start(f32[32,4,1]{0,2,1:T(1,128)} %get-tuple-element.122), channel_id=1, source_target_pairs={{0,1},{1,2},{2,3},{3,4},{4,5},{5,6},{6,7},{8,9},{9,10},{10,11},{11... | collective-permute-start | bytes 1544 | tf_op jit(solution)/shard_map/ppermute | solution.py:21
  296.0 20.2 %collective-permute-start.46 = (f32[1,32,2,16]{1,3,2,0:T(8,128)S(1)}, f32[1,32,2,16]{1,3,2,0:T(8,128)S(1)}, u32[]{:S(2)}, u32[]{:S(2)}) collective-permute-start(f32[1,32,2,16]{1,3,2,0:T(8,128)S(1)} %get-tuple-element.129), channel_id=1, source_target_pairs={{0,64},{64,0},{8,72},{72,8},{16,80},{80,16},{24,88},{88,24},{32,96... | collective-permute-start | bytes 12296 | tf_op jit(solution)/shard_map/ppermute | solution.py:43
  (96 other events, 1074.0 us)
where the time goes:
time: 508 us; the launch traced here: 502 us
  starting transfers between devices  256 us (50%)
  other arithmetic  101 us (20%)
  waiting for transfers between devices  73.7 us (15%)
  local copies, waits for them, and re-layouts  69.9 us (14%)
    ppermute x24, starting transfers between devices, with_halo(): lax.ppermute(tail, axis, [(i, (i + 1) % count) for i in range(ends)])  98.5 us
    ppermute x24, starting transfers between devices, from_behind(): lax.ppermute(value, axis, [(source, source + steps) for source in range(i...  66 us
    ppermute x24, starting transfers between devices, with_halo(): lax.ppermute(head, axis, [((i + 1) % count, i) for i in range(ends)])  49.3 us
    ppermute x8, starting transfers between devices, partner_2(): return lax.ppermute(block, axis, route)  42 us
    ppermute x24, waiting for transfers between devices, with_halo(): lax.ppermute(head, axis, [((i + 1) % count, i) for i in range(ends)])  39.7 us
    ppermute x24, waiting for transfers between devices, from_behind(): lax.ppermute(value, axis, [(source, source + steps) for source in range(i...  33.2 us
    reduce_sum x15, other arithmetic, restrict(): jnp.mean(field.reshape(depth, first // 2, 2, second // 2, 2), axis=(2, 4))  24.7 us
    unnamed x94, local copies, waits for them, and re-layouts  18.4 us
  transfers between devices with their start and end apart: 80, of which 23 were waited for; matrix products, arithmetic and copies ran while one was open for 22% of the time, Pallas kernels for 0%

commit v1 on v0

v1 whole, which is shorter than its diff:
```python
import jax
import jax.numpy as jnp
from jax import lax
from jax.experimental import pallas as pl
from jax.experimental.pallas import tpu as pltpu
from jax.sharding import PartitionSpec as P


MESH = pl.DeviceIdType.MESH
F32 = jnp.float32
WEIGHT = 0.8
NZ = 32
LANES = 128
SPAN = 64
WIDTH = 8
ROWS = (12, 8, 6, 12, 6, 9)
TILES = (6, 3, 2, 1, 1, 1)
GRID_ROWS = (512, 256, 128, 64, 32, 16)
N_SEMS = 80


class Level:
    def __init__(self, index, refs, base, width_at):
        self.index, self.base, self.width_at = index, base, width_at
        self.tiles = TILES[index]
        self.conduct, self.binding, self.source, self.smooth, self.fx, self.fy, self.fz, self.weight, self.work = refs
        self.scale = 0.25**index

    def cut(self, row):
        at = lax.rem(self.base + (row + 1 + GRID_ROWS[self.index]), GRID_ROWS[self.index])
        return jnp.where(at == 0, 0.0, 2.0 * self.scale).astype(F32)

    def y_factor(self, tile):
        halo, own = LANES >> self.index, 512 >> self.index
        low, high = halo - 1, halo + own - 1
        full = jnp.full((NZ, LANES), 2.0 * self.scale, F32)
        lane = lax.broadcasted_iota(jnp.int32, (NZ, LANES), 1)
        for place, edge in ((low, 0), (high, WIDTH - 1)):
            if place // LANES == tile:
                spot = jnp.where(self.width_at == edge, place % LANES, -1)
                full = jnp.where(lane == spot, 0.0, full)
        return full

    def z_factor(self):
        depth = lax.broadcasted_iota(jnp.int32, (NZ, LANES), 0)
        return jnp.where(depth == NZ - 1, 0.0, 2.0 * self.scale)


def tile_of(ref, row, tile):
    return ref[row, :, pl.ds(tile * LANES, LANES)]


def put(ref, row, tile, value):
    ref[row, :, pl.ds(tile * LANES, LANES)] = value


def for_rows(first, last, body, unrolled):
    if unrolled:
        for row in range(first, last):
            body(row)
    else:
        lax.fori_loop(first, last, lambda row, carry: (body(row), carry)[1], 0)


def lane_above(tiles, tile):
    here = tiles[tile]
    after = tiles[min(tile + 1, len(tiles) - 1)]
    lane = lax.broadcasted_iota(jnp.int32, here.shape, 1)
    return pltpu.roll(jnp.where(lane == 0, after, here), LANES - 1, 1)


def lane_below(tiles, tile):
    here = tiles[tile]
    before = tiles[max(tile - 1, 0)]
    lane = lax.broadcasted_iota(jnp.int32, here.shape, 1)
    return pltpu.roll(jnp.where(lane == LANES - 1, before, here), 1, 1)


def depth_above(value):
    return pltpu.roll(value, NZ - 1, 0)


def depth_below(value):
    return pltpu.roll(value, 1, 0)


def mean_face(factor, first, second):
    return factor * (first * second) / (first + second)


def faces(level, first, last, unrolled):
    def x_faces(row):
        factor = level.cut(row)
        for tile in range(level.tiles):
            put(level.fx, row, tile, mean_face(factor, tile_of(level.conduct, row, tile), tile_of(level.conduct, row + 1, tile)))

    def one(row):
        x_faces(row)
        cells = [tile_of(level.conduct, row, tile) for tile in range(level.tiles)]
        beside = [mean_face(level.y_factor(tile), cells[tile], lane_above(cells, tile)) for tile in range(level.tiles)]
        for tile in range(level.tiles):
            deep = mean_face(level.z_factor(), cells[tile], depth_above(cells[tile]))
            diagonal = tile_of(level.fx, row - 1, tile) + tile_of(level.fx, row, tile)
            diagonal = diagonal + lane_below(beside, tile) + beside[tile]
            diagonal = diagonal + depth_below(deep) + deep + level.scale * tile_of(level.binding, row, tile)
            put(level.fy, row, tile, beside[tile])
            put(level.fz, row, tile, deep)
            put(level.weight, row, tile, WEIGHT / diagonal)

    x_faces(first - 1)
    for_rows(first, last, one, unrolled)


def smooth(level, first, last, unrolled):
    def one(row):
        for tile in range(level.tiles):
            put(level.smooth, row, tile, tile_of(level.weight, row, tile) * tile_of(level.source, row, tile))

    for_rows(first, last, one, unrolled)


def residual(level, field, row):
    cells = [tile_of(field, row, tile) for tile in range(level.tiles)]
    along = [tile_of(level.fy, row, tile) * (lane_above(cells, tile) - cells[tile]) for tile in range(level.tiles)]
    out = []
    for tile in range(level.tiles):
        here = cells[tile]
        deep = tile_of(level.fz, row, tile) * (depth_above(here) - here)
        value = tile_of(level.source, row, tile) - level.scale * tile_of(level.binding, row, tile) * here
        value = value + tile_of(level.fx, row, tile) * (tile_of(field, row + 1, tile) - here)
        value = value - tile_of(level.fx, row - 1, tile) * (here - tile_of(field, row - 1, tile))
        value = value + (along[tile] - lane_below(along, tile)) + (deep - depth_below(deep))
        out.append(value)
    return out


def relax(level, field, first, last, store, unrolled):
    def one(row):
        rest = residual(level, field, row)
        for tile in range(level.tiles):
            store(row, tile, tile_of(field, row, tile) + tile_of(level.weight, row, tile) * rest[tile])

    for_rows(first, last, one, unrolled)


def exact_dot(value, selector):
    high = value.astype(jnp.bfloat16)
    left = value - high.astype(F32)
    middle = left.astype(jnp.bfloat16)
    low = (left - middle.astype(F32)).astype(jnp.bfloat16)
    total = jnp.dot(low, selector, preferred_element_type=F32) + jnp.dot(middle, selector, preferred_element_type=F32)
    return total + jnp.dot(high, selector, preferred_element_type=F32)


def coarsen(tiles_in, coarse_tiles, select):
    out = []
    for tile in range(coarse_tiles):
        if 2 * tile + 1 < len(tiles_in):
            pair = jnp.concatenate([tiles_in[2 * tile], tiles_in[2 * tile + 1]], axis=1)
            out.append(exact_dot(pair, select[0]))
        else:
            out.append(exact_dot(tiles_in[2 * tile], select[1]))
    return out


def kernel(right_ref, conduct_ref, binding_ref, out_ref, *scratch):
    levels_refs, (raw, raw_out, local_sem, coarse_send, coarse_recv) = scratch[:-5], scratch[-5:]
    loads = []
    for i, ref in enumerate((conduct_ref, right_ref, binding_ref)):
        for t in range(4):
            loads.append(pltpu.make_async_copy(ref.at[:, pl.ds(t * LANES, LANES)], raw.at[i, t], local_sem.at[4 * i + t]))
            loads[-1].start()
    span_at, width_at = lax.axis_index("span"), lax.axis_index("width")
    plane, across = span_at // 4, lax.rem(span_at, 4)
    d0, sb0, db1, s1, db2, s2, db3, s3, db5, s5 = levels_refs[:10]
    rest = list(levels_refs[10:])

    def take():
        return rest.pop(0)

    base = (8 * span_at - 2, 4 * span_at - 2, 2 * span_at - 2, 4 * plane - 4, 2 * plane - 2, plane - 4)
    d4, b4, s4 = take(), take(), take()
    own = [
        (d0, sb0.at[1], sb0.at[0]),
        (db1.at[0], db1.at[1], s1),
        (db2.at[0], db2.at[1], s2),
        (db3.at[0], db3.at[1], s3),
        (d4, b4, s4),
        (db5.at[0], db5.at[1], s5),
    ]
    levels = [Level(i, own[i] + tuple(take() for _ in range(6)), base[i], width_at) for i in range(6)]
    sums = take()
    lifts = take()
    iterates = [take() for _ in range(6)]

    def device(across_span, across_width=0):
        return (lax.rem(span_at + (across_span + SPAN), SPAN), lax.rem(width_at + (across_width + WIDTH), WIDTH))

    ring = [(dz, dx) for dz in (0, 1, -1) for dx in range(4) if (dz, dx) != (0, 0)]

    def ring_device(dz, dx):
        to = lax.rem(across + dx, 4)
        return (lax.rem(4 * plane + (4 * dz + SPAN) + to, SPAN), width_at)

    around = [(1, 0), (-1, 0), (0, 1), (0, -1), (1, 1), (1, -1), (-1, 1), (-1, -1)]
    far = [(dz, 0) for dz in (2, -2, 3, -3, 4, -4)]

    barrier = pltpu.get_barrier_semaphore()
    partners = [ring_device(dz, dx) for dz, dx in ring] + [device(4 * dz) for dz, _ in far]
    partners += [device(a, b) for a, b in around if b != 0]
    for partner in partners:
        pl.semaphore_signal(barrier, inc=1, device_id=partner, device_id_type=MESH)

    lane = lax.broadcasted_iota(jnp.int32, (2 * LANES, LANES), 0) // 2
    column = lax.broadcasted_iota(jnp.int32, (2 * LANES, LANES), 1)
    pair_select = jnp.where(lane == column, 0.25, 0.0).astype(jnp.bfloat16)
    lane = lax.broadcasted_iota(jnp.int32, (LANES, LANES), 0) // 2
    column = lax.broadcasted_iota(jnp.int32, (LANES, LANES), 1)
    twice_select = jnp.where(lane == lax.rem(column, LANES // 2), 0.25, 0.0).astype(jnp.bfloat16)
    select = (pair_select, twice_select)
    lane = lax.broadcasted_iota(jnp.int32, (LANES, LANES), 0)
    column = lax.broadcasted_iota(jnp.int32, (LANES, LANES), 1) // 2
    spread = tuple(jnp.where(lane == column + half * (LANES // 2), 1.0, 0.0).astype(jnp.bfloat16) for half in (0, 1))

    for i, ref in enumerate((d0, sb0.at[0], sb0.at[1])):
        for t in range(4):
            loads[4 * i + t].wait()
            for row in range(8):
                put(ref, 2 + row, 1 + t, raw[i, t, pl.ds(row, NZ, stride=8), :])

    pl.semaphore_wait(barrier, len(partners))

    copies = []

    def send(source, target, to):
        at = len(copies)
        copy = pltpu.make_async_remote_copy(
            src_ref=source, dst_ref=target, send_sem=coarse_send.at[at], recv_sem=coarse_recv.at[at], device_id=to, device_id_type=MESH
        )
        copy.start()
        copies.append(copy)
        return copy

    def arrive(group):
        for copy in group:
            copy.wait_recv()

    first = []
    for a, b in around:
        lanes_from, lanes_to = {0: (pl.ds(LANES, 4 * LANES),) * 2, 1: (pl.ds(4 * LANES, LANES), pl.ds(0, LANES)), -1: (pl.ds(LANES, LANES), pl.ds(5 * LANES, LANES))}[b]
        from_2, to_2 = {0: (pl.ds(2, 8),) * 2, 1: (pl.ds(8, 2), pl.ds(0, 2)), -1: (pl.ds(2, 2), pl.ds(10, 2))}[a]
        from_1, to_1 = {0: (pl.ds(2, 8),) * 2, 1: (pl.ds(9, 1), pl.ds(1, 1)), -1: (pl.ds(2, 1), pl.ds(10, 1))}[a]
        first.append(send(d0.at[from_2, :, lanes_from], d0.at[to_2, :, lanes_to], device(a, b)))
        first.append(send(sb0.at[:, from_1, :, lanes_from], sb0.at[:, to_1, :, lanes_to], device(a, b)))
    arrive(first)

    def coarse_fields(fine, coarse, n_rows, fine_row, coarse_row, fill_rows=None):
        for pick_fine, pick_coarse in ((fine.conduct, coarse.conduct), (fine.binding, coarse.binding)):
            tiles = [
                jnp.concatenate([tile_of(pick_fine, fine_row + 2 * i, t) + tile_of(pick_fine, fine_row + 2 * i + 1, t) for i in range(n_rows)], axis=0)
                for t in range(fine.tiles)
            ]
            for t, value in enumerate(coarsen(tiles, coarse.tiles, select)):
                for i in range(n_rows):
                    put(pick_coarse, coarse_row + i, t, value[i * NZ : (i + 1) * NZ])

    def coarse_source(fine, coarse, n_rows, fine_row, coarse_row, unrolled):
        def one(i):
            low = residual(fine, fine.smooth, fine_row + 2 * i)
            high = residual(fine, fine.smooth, fine_row + 2 * i + 1)
            for t in range(fine.tiles):
                put(sums, i, t, low[t] + high[t])

        for_rows(0, n_rows, one, unrolled)
        tiles = [jnp.concatenate([tile_of(sums, i, t) for i in range(n_rows)], axis=0) for t in range(fine.tiles)]
        for t, value in enumerate(coarsen(tiles, coarse.tiles, select)):
            for i in range(n_rows):
                put(coarse.source, coarse_row + i, t, value[i * NZ : (i + 1) * NZ])

    l0, l1, l2, l3, l4, l5 = levels

    coarse_fields(l0, l1, 4, 2, 2)
    fields_1 = []
    for to, d_from, d_to, b_from, b_to in ((1, 4, 0, 5, 1), (-1, 2, 6, 2, 6)):
        fields_1.append(send(db1.at[0, pl.ds(d_from, 2)], db1.at[0, pl.ds(d_to, 2)], device(to)))
        fields_1.append(send(db1.at[1, pl.ds(b_from, 1)], db1.at[1, pl.ds(b_to, 1)], device(to)))
    coarse_fields(l1, l2, 2, 2, 2)
    fields_2 = []
    for to, d_from, d_to, b_from, b_to in ((1, 2, 0, 3, 1), (-1, 2, 4, 2, 4)):
        fields_2.append(send(db2.at[0, pl.ds(d_from, 2)], db2.at[0, pl.ds(d_to, 2)], device(to)))
        fields_2.append(send(db2.at[1, pl.ds(b_from, 1)], db2.at[1, pl.ds(b_to, 1)], device(to)))
    mine = 4 + across
    coarse_fields(l2, l3, 1, 2, mine)
    fields_3 = [
        send(db3.at[:, pl.ds(mine, 1)], db3.at[:, pl.ds(4 * (1 - dz) + across, 1)], ring_device(dz, dx)) for dz, dx in ring
    ]

    faces(l0, 1, 11, False)
    smooth(l0, 1, 11, False)
    coarse_source(l0, l1, 4, 2, 2, False)

    sources_1 = [send(s1.at[pl.ds(5, 1)], s1.at[pl.ds(1, 1)], device(1)), send(s1.at[pl.ds(2, 1)], s1.at[pl.ds(6, 1)], device(-1))]
    arrive(fields_1)
    faces(l1, 1, 7, False)
    arrive(fields_3)
    coarse_fields(l3, l4, 6, 0, 0)
    coarse_fields(l4, l5, 1, 2, 4)
    fields_5 = [
        send(db5.at[:, pl.ds(4, 1)], db5.at[:, pl.ds(4 - dz, 1)], device(4 * dz)) for dz in (1, -1, 2, -2, 3, -3, 4, -4)
    ]
    arrive(sources_1)
    smooth(l1, 1, 7, False)
    coarse_source(l1, l2, 2, 2, 2, False)

    sources_2 = [send(s2.at[pl.ds(3, 1)], s2.at[pl.ds(1, 1)], device(1)), send(s2.at[pl.ds(2, 1)], s2.at[pl.ds(4, 1)], device(-1))]
    smooths_1 = [send(l1.smooth.at[pl.ds(4, 1)], l1.smooth.at[pl.ds(0, 1)], device(1)), send(l1.smooth.at[pl.ds(3, 1)], l1.smooth.at[pl.ds(7, 1)], device(-1))]
    arrive(fields_2)
    faces(l2, 1, 5, True)
    arrive(sources_2)
    smooth(l2, 1, 5, True)
    coarse_source(l2, l3, 1, 2, mine, True)

    sources_3 = [
        send(s3.at[pl.ds(mine, 1)], s3.at[pl.ds(4 * (1 - dz) + across, 1)], ring_device(dz, dx)) for dz, dx in ring
    ]
    smooths_2 = [send(l2.smooth.at[pl.ds(2, 1)], l2.smooth.at[pl.ds(0, 1)], device(1)), send(l2.smooth.at[pl.ds(3, 1)], l2.smooth.at[pl.ds(5, 1)], device(-1))]
    faces(l3, 1, 11, False)
    faces(l4, 1, 5, True)
    arrive(sources_3)
    smooth(l3, 1, 11, True)
    coarse_source(l3, l4, 4, 2, 1, False)
    smooth(l4, 1, 5, True)
    coarse_source(l4, l5, 1, 2, 4, True)

    sources_5 = [send(s5.at[pl.ds(4, 1)], s5.at[pl.ds(4 - dz, 1)], device(4 * dz)) for dz in (1, -1, 2, -2, 3, -3)]
    smooths_4 = [send(l4.smooth.at[pl.ds(2, 1)], l4.smooth.at[pl.ds(0, 1)], device(-4 * -1)), send(l4.smooth.at[pl.ds(3, 1)], l4.smooth.at[pl.ds(5, 1)], device(-4))]
    arrive(fields_5)
    faces(l5, 1, 8, True)
    arrive(sources_5)

    smooth(l5, 1, 8, True)

    def into(ref):
        return lambda row, tile, value: put(ref, row, tile, value)

    relax(l5, l5.smooth, 2, 7, into(l5.work), True)
    relax(l5, l5.work, 3, 6, into(iterates[5]), True)

    def lift(fine, coarse_ref, coarse_rows, coarse_tiles, first_row, last_row, coarse_of):
        values = [jnp.concatenate([tile_of(coarse_ref, c, t) for c in coarse_rows], axis=0) for t in range(coarse_tiles)]
        for t in range(fine.tiles):
            spread_out = exact_dot(values[t // 2], spread[t % 2])
            for row in range(first_row, last_row):
                at = coarse_of(row)
                put(lifts, row, t, tile_of(fine.smooth, row, t) + spread_out[at * NZ : (at + 1) * NZ])

    arrive(smooths_4)
    lift(l4, iterates[5], range(3, 6), 1, 0, 6, lambda row: row // 2)
    relax(l4, lifts, 1, 5, into(iterates[4]), True)
    lift(l3, iterates[4], range(1, 5), 1, 2, 10, lambda row: row // 2 - 1)
    relax(l3, lifts, 3, 9, into(iterates[3]), True)
    arrive(smooths_2)
    lift(l2, iterates[3], [across + 3 + i for i in range(3)], 1, 0, 6, lambda row: row // 2)
    relax(l2, lifts, 1, 5, into(iterates[2]), True)
    arrive(smooths_1)
    lift(l1, iterates[2], range(1, 5), 2, 0, 8, lambda row: row // 2)
    relax(l1, lifts, 1, 7, into(iterates[1]), False)
    lift(l0, iterates[1], range(1, 7), 3, 1, 11, lambda row: (row - 2) // 2 + 1)

    def finish(row, tile, value):
        if 1 <= tile <= 4:
            raw_out[tile - 1, pl.ds(row - 2, NZ, stride=8), :] = value

    relax(l0, lifts, 2, 10, finish, False)
    stores = []
    for t in range(4):
        stores.append(pltpu.make_async_copy(raw_out.at[t], out_ref.at[:, pl.ds(t * LANES, LANES)], local_sem.at[t]))
        stores[-1].start()
    for copy in stores:
        copy.wait()

    for copy in copies:
        copy.wait_send()


def shapes():
    def rows(level, *lead):
        return pltpu.VMEM((*lead, ROWS[level], NZ, TILES[level] * LANES), F32)

    first = [rows(0), rows(0, 2), rows(1, 2), rows(1), rows(2, 2), rows(2), rows(3, 2), rows(3), rows(5, 2), rows(5)]
    first += [rows(4), rows(4), rows(4)]
    for level in range(6):
        first += [rows(level) for _ in range(6)]
    first += [pltpu.VMEM((4, NZ, TILES[0] * LANES), F32), pltpu.VMEM((12, NZ, TILES[0] * LANES), F32)]
    first += [rows(level) for level in range(6)]
    first += [pltpu.VMEM((3, 4, NZ * 8, LANES), F32), pltpu.VMEM((4, NZ * 8, LANES), F32), pltpu.SemaphoreType.DMA((12,))]
    return first + [pltpu.SemaphoreType.DMA((N_SEMS,)), pltpu.SemaphoreType.DMA((N_SEMS,))]


def on_device(right_side, diffusivity, reaction):
    flat = [field.reshape(NZ * 8, 512) for field in (right_side, diffusivity, reaction)]
    out = pl.pallas_call(
        kernel,
        out_shape=jax.ShapeDtypeStruct((NZ * 8, 512), F32),
        in_specs=[pl.BlockSpec(memory_space=pl.ANY)] * 3,
        out_specs=pl.BlockSpec(memory_space=pl.ANY),
        scratch_shapes=shapes(),
        compiler_params=pltpu.CompilerParams(collective_id=0, has_side_effects=True, vmem_limit_bytes=48 << 20),
    )(*flat)
    return out.reshape(NZ, 8, 512)


def solution(mesh):
    specs = P(None, "span", "width")
    return jax.shard_map(on_device, mesh=mesh, in_specs=(specs,) * 3, out_specs=specs, check_vma=False)
```

time: 508 us -> 71.2 us (0.14)
  the two profiles are of different devices: /device:TPU:15 before, /device:TPU:6 now
where the time goes in v1:
time: 71.2 us; the launch traced here: 70.9 us
  Pallas kernels  67 us (94%)
  local copies, waits for them, and re-layouts  3.92 us (6%)
    pallas_call x1, Pallas kernels, on_device(): pl.pallas_call(kernel, out_shape=jax.ShapeDtypeStruct((NZ * 8, 512), F32)...  67 us
    unnamed x7, local copies, waits for them, and re-layouts  3.92 us

profile of v1, /device:TPU:6, one launch (start us, length us, event | category | flops | bytes accessed | tf_op | source)
XLA Modules:
  0.0 70.9 jit_solution(7365338883350339854)
XLA Ops:
  0.0 0.0 copy-start
  0.0 1.0 %copy-done = f32[32,8,512]{2,1,0:T(8,128)S(1)} copy-done((f32[32,8,512]{2,1,0:T(8,128)S(1)}, f32[32,8,512]{2,1,0:T(8,128)}, u32[]{:S(2)}) %copy-start) | copy-done | bytes 524312
  1.0 0.0 copy-start.1
  1.0 1.0 %copy-done.1 = f32[32,8,512]{2,1,0:T(8,128)S(1)} copy-done((f32[32,8,512]{2,1,0:T(8,128)S(1)}, f32[32,8,512]{2,1,0:T(8,128)}, u32[]{:S(2)}) %copy-start.1) | copy-done | bytes 524312
  2.1 0.0 copy-start.2
  2.1 1.0 %copy-done.2 = f32[32,8,512]{2,1,0:T(8,128)S(1)} copy-done((f32[32,8,512]{2,1,0:T(8,128)S(1)}, f32[32,8,512]{2,1,0:T(8,128)}, u32[]{:S(2)}) %copy-start.2) | copy-done | bytes 524312
  3.1 67.0 %shard_map.37 = f32[256,512]{1,0:T(8,128)S(1)} custom-call(f32[256,512]{1,0:T(8,128)S(1)} %bitcast.5, f32[256,512]{1,0:T(8,128)S(1)} %bitcast.6, f32[256,512]{1,0:T(8,128)S(1)} %bitcast.7), custom_call_target="tpu_custom_call" | custom-call | tf_op jit(solution)/shard_map/pallas_call | solution.py:402
  70.1 0.8 %copy.5 = f32[32,8,512]{2,1,0:T(8,128)} copy(f32[32,8,512]{2,1,0:T(8,128)S(1)} %bitcast.4) | data formatting | bytes 1048576
Async XLA Ops:
  0.0 1.0 %copy-start = (f32[32,8,512]{2,1,0:T(8,128)S(1)}, f32[32,8,512]{2,1,0:T(8,128)}, u32[]{:S(2)}) copy-start(f32[32,8,512]{2,1,0:T(8,128)} %param.3) | copy-start | bytes 1572868
  1.0 1.0 %copy-start.1 = (f32[32,8,512]{2,1,0:T(8,128)S(1)}, f32[32,8,512]{2,1,0:T(8,128)}, u32[]{:S(2)}) copy-start(f32[32,8,512]{2,1,0:T(8,128)} %param.4) | copy-start | bytes 1572868
  2.1 1.0 %copy-start.2 = (f32[32,8,512]{2,1,0:T(8,128)S(1)}, f32[32,8,512]{2,1,0:T(8,128)}, u32[]{:S(2)}) copy-start(f32[32,8,512]{2,1,0:T(8,128)} %param.5) | copy-start | bytes 1572868

commit v2 on v1

--- a/solution.py
+++ b/solution.py
@@ -16,7 +16,8 @@
 ROWS = (12, 8, 6, 12, 6, 9)
 TILES = (6, 3, 2, 1, 1, 1)
 GRID_ROWS = (512, 256, 128, 64, 32, 16)
-N_SEMS = 80
+N_SEMS = 96
+VMEM_BYTES = 62 << 20
 
 
 class Level:
@@ -41,6 +42,9 @@
                 full = jnp.where(lane == spot, 0.0, full)
         return full
 
+    def y_factors(self):
+        return [self.y_factor(tile) for tile in range(self.tiles)]
+
     def z_factor(self):
         depth = lax.broadcasted_iota(jnp.int32, (NZ, LANES), 0)
         return jnp.where(depth == NZ - 1, 0.0, 2.0 * self.scale)
@@ -88,26 +92,46 @@
     return factor * (first * second) / (first + second)
 
 
+def face_x(level, row, tiles):
+    factor = level.cut(row)
+    for tile in tiles:
+        put(level.fx, row, tile, mean_face(factor, tile_of(level.conduct, row, tile), tile_of(level.conduct, row + 1, tile)))
+
+
+def face_y(level, row, tiles, factors):
+    for tile in tiles:
+        near = {t: tile_of(level.conduct, row, t) for t in {tile, min(tile + 1, level.tiles - 1)}}
+        after = near[min(tile + 1, level.tiles - 1)]
+        put(level.fy, row, tile, mean_face(factors[tile], near[tile], lane_above((near[tile], after), 0)))
+
+
+def face_z(level, row, tiles, factor):
+    for tile in tiles:
+        here = tile_of(level.conduct, row, tile)
+        put(level.fz, row, tile, mean_face(factor, here, depth_above(here)))
+
+
+def weigh(level, row, tiles):
+    for tile in tiles:
+        beside, deep = tile_of(level.fy, row, tile), tile_of(level.fz, row, tile)
+        before = tile_of(level.fy, row, max(tile - 1, 0))
+        diagonal = tile_of(level.fx, row - 1, tile) + tile_of(level.fx, row, tile)
+        diagonal = diagonal + lane_below((before, beside), 1) + beside
+        diagonal = diagonal + depth_below(deep) + deep + level.scale * tile_of(level.binding, row, tile)
+        put(level.weight, row, tile, WEIGHT / diagonal)
+
+
 def faces(level, first, last, unrolled):
-    def x_faces(row):
-        factor = level.cut(row)
-        for tile in range(level.tiles):
-            put(level.fx, row, tile, mean_face(factor, tile_of(level.conduct, row, tile), tile_of(level.conduct, row + 1, tile)))
+    tiles = range(level.tiles)
+    factors, deep_factor = level.y_factors(), level.z_factor()
 
     def one(row):
-        x_faces(row)
-        cells = [tile_of(level.conduct, row, tile) for tile in range(level.tiles)]
-        beside = [mean_face(level.y_factor(tile), cells[tile], lane_above(cells, tile)) for tile in range(level.tiles)]
-        for tile in range(level.tiles):
-            deep = mean_face(level.z_factor(), cells[tile], depth_above(cells[tile]))
-            diagonal = tile_of(level.fx, row - 1, tile) + tile_of(level.fx, row, tile)
-            diagonal = diagonal + lane_below(beside, tile) + beside[tile]
-            diagonal = diagonal + depth_below(deep) + deep + level.scale * tile_of(level.binding, row, tile)
-            put(level.fy, row, tile, beside[tile])
-            put(level.fz, row, tile, deep)
-            put(level.weight, row, tile, WEIGHT / diagonal)
-
-    x_faces(first - 1)
+        face_x(level, row, tiles)
+        face_y(level, row, tiles, factors)
+        face_z(level, row, tiles, deep_factor)
+        weigh(level, row, tiles)
+
+    face_x(level, first - 1, tiles)
     for_rows(first, last, one, unrolled)
 
 
@@ -164,12 +188,7 @@
 
 
 def kernel(right_ref, conduct_ref, binding_ref, out_ref, *scratch):
-    levels_refs, (raw, raw_out, local_sem, coarse_send, coarse_recv) = scratch[:-5], scratch[-5:]
-    loads = []
-    for i, ref in enumerate((conduct_ref, right_ref, binding_ref)):
-        for t in range(4):
-            loads.append(pltpu.make_async_copy(ref.at[:, pl.ds(t * LANES, LANES)], raw.at[i, t], local_sem.at[4 * i + t]))
-            loads[-1].start()
+    levels_refs, (staged, packed_fields, packed_source, local_sem, coarse_send, coarse_recv) = scratch[:-6], scratch[-6:]
     span_at, width_at = lax.axis_index("span"), lax.axis_index("width")
     plane, across = span_at // 4, lax.rem(span_at, 4)
     d0, sb0, db1, s1, db2, s2, db3, s3, db5, s5 = levels_refs[:10]
@@ -211,6 +230,13 @@
     for partner in partners:
         pl.semaphore_signal(barrier, inc=1, device_id=partner, device_id_type=MESH)
 
+    inner = pl.ds(LANES, 4 * LANES)
+    loads = []
+    for i, (ref, target) in enumerate(((conduct_ref, d0), (right_ref, sb0.at[0]), (binding_ref, sb0.at[1]))):
+        for row in range(8):
+            loads.append(pltpu.make_async_copy(ref.at[:, row, :], target.at[2 + row, :, inner], local_sem.at[8 * i + row]))
+            loads[-1].start()
+
     lane = lax.broadcasted_iota(jnp.int32, (2 * LANES, LANES), 0) // 2
     column = lax.broadcasted_iota(jnp.int32, (2 * LANES, LANES), 1)
     pair_select = jnp.where(lane == column, 0.25, 0.0).astype(jnp.bfloat16)
@@ -222,12 +248,6 @@
     column = lax.broadcasted_iota(jnp.int32, (LANES, LANES), 1) // 2
     spread = tuple(jnp.where(lane == column + half * (LANES // 2), 1.0, 0.0).astype(jnp.bfloat16) for half in (0, 1))
 
-    for i, ref in enumerate((d0, sb0.at[0], sb0.at[1])):
-        for t in range(4):
-            loads[4 * i + t].wait()
-            for row in range(8):
-                put(ref, 2 + row, 1 + t, raw[i, t, pl.ds(row, NZ, stride=8), :])
-
     pl.semaphore_wait(barrier, len(partners))
 
     copies = []
@@ -246,12 +266,42 @@
             copy.wait_recv()
 
     first = []
-    for a, b in around:
-        lanes_from, lanes_to = {0: (pl.ds(LANES, 4 * LANES),) * 2, 1: (pl.ds(4 * LANES, LANES), pl.ds(0, LANES)), -1: (pl.ds(LANES, LANES), pl.ds(5 * LANES, LANES))}[b]
-        from_2, to_2 = {0: (pl.ds(2, 8),) * 2, 1: (pl.ds(8, 2), pl.ds(0, 2)), -1: (pl.ds(2, 2), pl.ds(10, 2))}[a]
-        from_1, to_1 = {0: (pl.ds(2, 8),) * 2, 1: (pl.ds(9, 1), pl.ds(1, 1)), -1: (pl.ds(2, 1), pl.ds(10, 1))}[a]
-        first.append(send(d0.at[from_2, :, lanes_from], d0.at[to_2, :, lanes_to], device(a, b)))
-        first.append(send(sb0.at[:, from_1, :, lanes_from], sb0.at[:, to_1, :, lanes_to], device(a, b)))
+    for to, near, second in ((1, 7, 6), (-1, 0, 1)):
+        halo = 1 if to == 1 else 10
+        first.append(send(conduct_ref.at[:, near, :], d0.at[halo, :, inner], device(to)))
+        first.append(send(conduct_ref.at[:, second, :], d0.at[halo - to, :, inner], device(to)))
+        first.append(send(right_ref.at[:, near, :], sb0.at[0, halo, :, inner], device(to)))
+        first.append(send(binding_ref.at[:, near, :], sb0.at[1, halo, :, inner], device(to)))
+    for load in loads[:8]:
+        load.wait()
+
+    def sideways(source, spans):
+        for b in (1, -1):
+            lanes_from, lanes_to = (pl.ds(4 * LANES, LANES), pl.ds(0, LANES)) if b == 1 else (pl.ds(LANES, LANES), pl.ds(5 * LANES, LANES))
+            for a, rows_from, rows_to in spans:
+                first.append(send(source.at[..., rows_from, :, lanes_from], source.at[..., rows_to, :, lanes_to], device(a, b)))
+
+    sideways(d0, ((0, pl.ds(2, 8), pl.ds(2, 8)), (1, pl.ds(8, 2), pl.ds(0, 2)), (-1, pl.ds(2, 2), pl.ds(10, 2))))
+    for load in loads[8:]:
+        load.wait()
+    for field in (sb0.at[0], sb0.at[1]):
+        sideways(field, ((0, pl.ds(2, 8), pl.ds(2, 8)), (1, pl.ds(9, 1), pl.ds(1, 1)), (-1, pl.ds(2, 1), pl.ds(10, 1))))
+
+    l0, l1, l2, l3, l4, l5 = levels
+    factors_0, deep_0 = l0.y_factors(), l0.z_factor()
+
+    def inside(row):
+        face_x(l0, row, range(1, 5))
+        face_y(l0, row, range(1, 4), factors_0)
+        face_z(l0, row, range(1, 5), deep_0)
+
+        @pl.when(row > 2)
+        def _():
+            weigh(l0, row, (2, 3))
+
+    for_rows(2, 9, inside, False)
+    face_y(l0, 9, range(1, 4), factors_0)
+    face_z(l0, 9, range(1, 5), deep_0)
     arrive(first)
 
     def coarse_fields(fine, coarse, n_rows, fine_row, coarse_row, fill_rows=None):
@@ -277,13 +327,47 @@
             for i in range(n_rows):
                 put(coarse.source, coarse_row + i, t, value[i * NZ : (i + 1) * NZ])
 
-    l0, l1, l2, l3, l4, l5 = levels
+    def pack(value):
+        lane = lax.broadcasted_iota(jnp.int32, (8, LANES), 1) // 32
+        out = value[0:8]
+        for group in range(1, 4):
+            out = jnp.where(lane == group, pltpu.roll(value[8 * group : 8 * group + 8], 32 * group, 1), out)
+        return out
+
+    def unpack(value):
+        return jnp.concatenate([value] + [pltpu.roll(value, LANES - 32 * group, 1) for group in range(1, 4)], axis=0)
 
     coarse_fields(l0, l1, 4, 2, 2)
     fields_1 = []
     for to, d_from, d_to, b_from, b_to in ((1, 4, 0, 5, 1), (-1, 2, 6, 2, 6)):
         fields_1.append(send(db1.at[0, pl.ds(d_from, 2)], db1.at[0, pl.ds(d_to, 2)], device(to)))
         fields_1.append(send(db1.at[1, pl.ds(b_from, 1)], db1.at[1, pl.ds(b_to, 1)], device(to)))
+
+    def outside(row):
+        face_x(l0, row, (0, 5))
+        face_y(l0, row, (0, 4, 5), factors_0)
+        face_z(l0, row, (0, 5), deep_0)
+
+    for row in (0, 1, 9, 10):
+        face_x(l0, row, range(6))
+    for row in (1, 10):
+        face_y(l0, row, range(6), factors_0)
+        face_z(l0, row, range(6), deep_0)
+
+    def weigh_rim(row):
+        outside(row)
+        weigh(l0, row, (0, 1, 4, 5))
+
+    outside(2)
+    for_rows(3, 9, weigh_rim, False)
+    outside(9)
+    for row in (1, 2, 9, 10):
+        weigh(l0, row, range(6))
+    smooth(l0, 1, 11, False)
+    coarse_source(l0, l1, 4, 2, 2, False)
+
+    sources_1 = [send(s1.at[pl.ds(5, 1)], s1.at[pl.ds(1, 1)], device(1)), send(s1.at[pl.ds(2, 1)], s1.at[pl.ds(6, 1)], device(-1))]
+
     coarse_fields(l1, l2, 2, 2, 2)
     fields_2 = []
     for to, d_from, d_to, b_from, b_to in ((1, 2, 0, 3, 1), (-1, 2, 4, 2, 4)):
@@ -294,20 +378,8 @@
     fields_3 = [
         send(db3.at[:, pl.ds(mine, 1)], db3.at[:, pl.ds(4 * (1 - dz) + across, 1)], ring_device(dz, dx)) for dz, dx in ring
     ]
-
-    faces(l0, 1, 11, False)
-    smooth(l0, 1, 11, False)
-    coarse_source(l0, l1, 4, 2, 2, False)
-
-    sources_1 = [send(s1.at[pl.ds(5, 1)], s1.at[pl.ds(1, 1)], device(1)), send(s1.at[pl.ds(2, 1)], s1.at[pl.ds(6, 1)], device(-1))]
     arrive(fields_1)
     faces(l1, 1, 7, False)
-    arrive(fields_3)
-    coarse_fields(l3, l4, 6, 0, 0)
-    coarse_fields(l4, l5, 1, 2, 4)
-    fields_5 = [
-        send(db5.at[:, pl.ds(4, 1)], db5.at[:, pl.ds(4 - dz, 1)], device(4 * dz)) for dz in (1, -1, 2, -2, 3, -3, 4, -4)
-    ]
     arrive(sources_1)
     smooth(l1, 1, 7, False)
     coarse_source(l1, l2, 2, 2, 2, False)
@@ -324,6 +396,14 @@
         send(s3.at[pl.ds(mine, 1)], s3.at[pl.ds(4 * (1 - dz) + across, 1)], ring_device(dz, dx)) for dz, dx in ring
     ]
     smooths_2 = [send(l2.smooth.at[pl.ds(2, 1)], l2.smooth.at[pl.ds(0, 1)], device(1)), send(l2.smooth.at[pl.ds(3, 1)], l2.smooth.at[pl.ds(5, 1)], device(-1))]
+    arrive(fields_3)
+    coarse_fields(l3, l4, 6, 0, 0)
+    coarse_fields(l4, l5, 1, 2, 4)
+    for i in range(2):
+        packed_fields[i, 4] = pack(db5[i, 4])
+    fields_5 = [
+        send(packed_fields.at[:, pl.ds(4, 1)], packed_fields.at[:, pl.ds(4 - dz, 1)], device(4 * dz)) for dz in (1, -1, 2, -2, 3, -3, 4, -4)
+    ]
     faces(l3, 1, 11, False)
     faces(l4, 1, 5, True)
     arrive(sources_3)
@@ -332,11 +412,17 @@
     smooth(l4, 1, 5, True)
     coarse_source(l4, l5, 1, 2, 4, True)
 
-    sources_5 = [send(s5.at[pl.ds(4, 1)], s5.at[pl.ds(4 - dz, 1)], device(4 * dz)) for dz in (1, -1, 2, -2, 3, -3)]
-    smooths_4 = [send(l4.smooth.at[pl.ds(2, 1)], l4.smooth.at[pl.ds(0, 1)], device(-4 * -1)), send(l4.smooth.at[pl.ds(3, 1)], l4.smooth.at[pl.ds(5, 1)], device(-4))]
+    packed_source[4] = pack(s5[4])
+    sources_5 = [send(packed_source.at[pl.ds(4, 1)], packed_source.at[pl.ds(4 - dz, 1)], device(4 * dz)) for dz in (1, -1, 2, -2, 3, -3)]
+    smooths_4 = [send(l4.smooth.at[pl.ds(2, 1)], l4.smooth.at[pl.ds(0, 1)], device(4)), send(l4.smooth.at[pl.ds(3, 1)], l4.smooth.at[pl.ds(5, 1)], device(-4))]
     arrive(fields_5)
+    for row in (0, 1, 2, 3, 5, 6, 7, 8):
+        for i in range(2):
+            db5[i, row] = unpack(packed_fields[i, row])
     faces(l5, 1, 8, True)
     arrive(sources_5)
+    for row in (1, 2, 3, 5, 6, 7):
+        s5[row] = unpack(packed_source[row])
 
     smooth(l5, 1, 8, True)
 
@@ -369,16 +455,15 @@
 
     def finish(row, tile, value):
         if 1 <= tile <= 4:
-            raw_out[tile - 1, pl.ds(row - 2, NZ, stride=8), :] = value
+            put(staged, row - 2, tile - 1, value)
 
     relax(l0, lifts, 2, 10, finish, False)
     stores = []
-    for t in range(4):
-        stores.append(pltpu.make_async_copy(raw_out.at[t], out_ref.at[:, pl.ds(t * LANES, LANES)], local_sem.at[t]))
+    for row in range(8):
+        stores.append(pltpu.make_async_copy(staged.at[row], out_ref.at[:, row, :], local_sem.at[row]))
         stores[-1].start()
     for copy in stores:
         copy.wait()
-
     for copy in copies:
         copy.wait_send()
 
@@ -393,21 +478,19 @@
         first += [rows(level) for _ in range(6)]
     first += [pltpu.VMEM((4, NZ, TILES[0] * LANES), F32), pltpu.VMEM((12, NZ, TILES[0] * LANES), F32)]
     first += [rows(level) for level in range(6)]
-    first += [pltpu.VMEM((3, 4, NZ * 8, LANES), F32), pltpu.VMEM((4, NZ * 8, LANES), F32), pltpu.SemaphoreType.DMA((12,))]
+    first += [pltpu.VMEM((8, NZ, 512), F32), pltpu.VMEM((2, 9, 8, LANES), F32), pltpu.VMEM((9, 8, LANES), F32), pltpu.SemaphoreType.DMA((24,))]
     return first + [pltpu.SemaphoreType.DMA((N_SEMS,)), pltpu.SemaphoreType.DMA((N_SEMS,))]
 
 
 def on_device(right_side, diffusivity, reaction):
-    flat = [field.reshape(NZ * 8, 512) for field in (right_side, diffusivity, reaction)]
-    out = pl.pallas_call(
+    return pl.pallas_call(
         kernel,
-        out_shape=jax.ShapeDtypeStruct((NZ * 8, 512), F32),
+        out_shape=jax.ShapeDtypeStruct((NZ, 8, 512), F32),
         in_specs=[pl.BlockSpec(memory_space=pl.ANY)] * 3,
         out_specs=pl.BlockSpec(memory_space=pl.ANY),
         scratch_shapes=shapes(),
-        compiler_params=pltpu.CompilerParams(collective_id=0, has_side_effects=True, vmem_limit_bytes=48 << 20),
-    )(*flat)
-    return out.reshape(NZ, 8, 512)
+        compiler_params=pltpu.CompilerParams(collective_id=0, has_side_effects=True, vmem_limit_bytes=VMEM_BYTES),
+    )(right_side, diffusivity, reaction)
 
 
 def solution(mesh):

time: 71.2 us -> 63 us (0.88)
  Pallas kernels: 67 us -> 60.2 us
  local copies, waits for them, and re-layouts: 3.92 us -> 1.87 us
    pallas_call x1, Pallas kernels: 67 us -> 60.2 us  [on_device(): pl.pallas_call(kernel, out_shape=jax.ShapeDtypeStruct((NZ, 8, 512), F32),...]
    unnamed x7 -> x1, local copies, waits for them, and re-layouts: 3.92 us -> 1.87 us
where the time goes in v2:
time: 63 us; the launch traced here: 62.1 us
  Pallas kernels  60.2 us (96%)
  local copies, waits for them, and re-layouts  1.87 us (3%)
    pallas_call x1, Pallas kernels, on_device(): pl.pallas_call(kernel, out_shape=jax.ShapeDtypeStruct((NZ, 8, 512), F32),...  60.2 us
    unnamed x1, local copies, waits for them, and re-layouts  1.87 us

profile of v2, /device:TPU:6, one launch (start us, length us, event | category | flops | bytes accessed | tf_op | source)
XLA Modules:
  0.0 62.1 jit_solution(15040754846708158734)
XLA Ops:
  0.0 60.2 %shard_map.37 = f32[32,8,512]{2,1,0:T(8,128)} custom-call(f32[32,8,512]{2,1,0:T(8,128)} %right_ref.1, f32[32,8,512]{2,1,0:T(8,128)} %conduct_ref.1, f32[32,8,512]{2,1,0:T(8,128)} %binding_ref.1), custom_call_target="tpu_custom_call" | custom-call | tf_op jit(solution)/shard_map/pallas_call | solution.py:486
  60.2 1.9 %copy.5 = f32[32,8,512]{2,1,0:T(8,128)} copy(f32[32,8,512]{2,1,0:T(8,128)} %shard_map.37) | data formatting | bytes 1048576

commit v3 on v2

--- a/solution.py
+++ b/solution.py
@@ -63,7 +63,7 @@
         for row in range(first, last):
             body(row)
     else:
-        lax.fori_loop(first, last, lambda row, carry: (body(row), carry)[1], 0)
+        lax.fori_loop(first, last, lambda row, carry: (body(row), carry)[1], 0, unroll=2 if (last - first) % 2 == 0 else 1)
 
 
 def lane_above(tiles, tile):
@@ -143,11 +143,15 @@
     for_rows(first, last, one, unrolled)
 
 
-def residual(level, field, row):
+def residual(level, field, row, wanted=None):
+    wanted = wanted or range(level.tiles)
     cells = [tile_of(field, row, tile) for tile in range(level.tiles)]
-    along = [tile_of(level.fy, row, tile) * (lane_above(cells, tile) - cells[tile]) for tile in range(level.tiles)]
+    along = {
+        tile: tile_of(level.fy, row, tile) * (lane_above(cells, tile) - cells[tile])
+        for tile in range(max(wanted[0] - 1, 0), wanted[-1] + 1)
+    }
     out = []
-    for tile in range(level.tiles):
+    for tile in wanted:
         here = cells[tile]
         deep = tile_of(level.fz, row, tile) * (depth_above(here) - here)
         value = tile_of(level.source, row, tile) - level.scale * tile_of(level.binding, row, tile) * here
@@ -158,11 +162,11 @@
     return out
 
 
-def relax(level, field, first, last, store, unrolled):
+def relax(level, field, first, last, store, unrolled, wanted=None):
     def one(row):
-        rest = residual(level, field, row)
-        for tile in range(level.tiles):
-            store(row, tile, tile_of(field, row, tile) + tile_of(level.weight, row, tile) * rest[tile])
+        wanted_tiles = wanted or range(level.tiles)
+        for tile, rest in zip(wanted_tiles, residual(level, field, row, wanted)):
+            store(row, tile, tile_of(field, row, tile) + tile_of(level.weight, row, tile) * rest)
 
     for_rows(first, last, one, unrolled)
 
@@ -225,8 +229,8 @@
     far = [(dz, 0) for dz in (2, -2, 3, -3, 4, -4)]
 
     barrier = pltpu.get_barrier_semaphore()
-    partners = [ring_device(dz, dx) for dz, dx in ring] + [device(4 * dz) for dz, _ in far]
-    partners += [device(a, b) for a, b in around if b != 0]
+    partners = [device(a, b) for a, b in around if b != 0]
+    partners += [ring_device(dz, dx) for dz, dx in ring] + [device(4 * dz) for dz, _ in far]
     for partner in partners:
         pl.semaphore_signal(barrier, inc=1, device_id=partner, device_id_type=MESH)
 
@@ -304,15 +308,24 @@
     face_z(l0, 9, range(1, 5), deep_0)
     arrive(first)
 
-    def coarse_fields(fine, coarse, n_rows, fine_row, coarse_row, fill_rows=None):
-        for pick_fine, pick_coarse in ((fine.conduct, coarse.conduct), (fine.binding, coarse.binding)):
-            tiles = [
-                jnp.concatenate([tile_of(pick_fine, fine_row + 2 * i, t) + tile_of(pick_fine, fine_row + 2 * i + 1, t) for i in range(n_rows)], axis=0)
-                for t in range(fine.tiles)
-            ]
-            for t, value in enumerate(coarsen(tiles, coarse.tiles, select)):
-                for i in range(n_rows):
-                    put(pick_coarse, coarse_row + i, t, value[i * NZ : (i + 1) * NZ])
+    def coarse_field(fine, coarse, n_rows, fine_row, coarse_row):
+        tiles = [
+            jnp.concatenate([tile_of(fine[0], fine_row + 2 * i, t) + tile_of(fine[0], fine_row + 2 * i + 1, t) for i in range(n_rows)], axis=0)
+            for t in range(fine[1])
+        ]
+        for t, value in enumerate(coarsen(tiles, coarse[1], select)):
+            for i in range(n_rows):
+                put(coarse[0], coarse_row + i, t, value[i * NZ : (i + 1) * NZ])
+
+    def coarse_conduct(fine, coarse, n_rows, fine_row, coarse_row):
+        coarse_field((fine.conduct, fine.tiles), (coarse.conduct, coarse.tiles), n_rows, fine_row, coarse_row)
+
+    def coarse_binding(fine, coarse, n_rows, fine_row, coarse_row):
+        coarse_field((fine.binding, fine.tiles), (coarse.binding, coarse.tiles), n_rows, fine_row, coarse_row)
+
+    def coarse_fields(fine, coarse, n_rows, fine_row, coarse_row):
+        coarse_conduct(fine, coarse, n_rows, fine_row, coarse_row)
+        coarse_binding(fine, coarse, n_rows, fine_row, coarse_row)
 
     def coarse_source(fine, coarse, n_rows, fine_row, coarse_row, unrolled):
         def one(i):
@@ -337,10 +350,11 @@
     def unpack(value):
         return jnp.concatenate([value] + [pltpu.roll(value, LANES - 32 * group, 1) for group in range(1, 4)], axis=0)
 
-    coarse_fields(l0, l1, 4, 2, 2)
+    coarse_conduct(l0, l1, 6, 0, 1)
+    coarse_binding(l0, l1, 4, 2, 2)
     fields_1 = []
-    for to, d_from, d_to, b_from, b_to in ((1, 4, 0, 5, 1), (-1, 2, 6, 2, 6)):
-        fields_1.append(send(db1.at[0, pl.ds(d_from, 2)], db1.at[0, pl.ds(d_to, 2)], device(to)))
+    for to, d_from, d_to, b_from, b_to in ((1, 4, 0, 5, 1), (-1, 3, 7, 2, 6)):
+        fields_1.append(send(db1.at[0, pl.ds(d_from, 1)], db1.at[0, pl.ds(d_to, 1)], device(to)))
         fields_1.append(send(db1.at[1, pl.ds(b_from, 1)], db1.at[1, pl.ds(b_to, 1)], device(to)))
 
     def outside(row):
@@ -370,22 +384,38 @@
 
     coarse_fields(l1, l2, 2, 2, 2)
     fields_2 = []
-    for to, d_from, d_to, b_from, b_to in ((1, 2, 0, 3, 1), (-1, 2, 4, 2, 4)):
-        fields_2.append(send(db2.at[0, pl.ds(d_from, 2)], db2.at[0, pl.ds(d_to, 2)], device(to)))
+    for to, d_from, d_to, b_from, b_to in ((1, 2, 0, 3, 1), (-1, 3, 5, 2, 4)):
+        fields_2.append(send(db2.at[0, pl.ds(d_from, 1)], db2.at[0, pl.ds(d_to, 1)], device(to)))
         fields_2.append(send(db2.at[1, pl.ds(b_from, 1)], db2.at[1, pl.ds(b_to, 1)], device(to)))
+    factors_1, deep_1 = l1.y_factors(), l1.z_factor()
+    for row in (2, 3, 4, 5):
+        face_y(l1, row, range(3), factors_1)
+        face_z(l1, row, range(3), deep_1)
+    for row in (1, 2, 3, 4, 5):
+        face_x(l1, row, range(3))
+    for row in (1, 6):
+        face_y(l1, row, range(3), factors_1)
+        face_z(l1, row, range(3), deep_1)
+    for row in (3, 4):
+        weigh(l1, row, range(3))
     mine = 4 + across
     coarse_fields(l2, l3, 1, 2, mine)
+    arrive(fields_1)
+    for row in (0, 6):
+        face_x(l1, row, range(3))
+    for row in (1, 2, 5, 6):
+        weigh(l1, row, range(3))
+    coarse_conduct(l1, l2, 1, 0, 1)
+    coarse_conduct(l1, l2, 1, 6, 4)
+    arrive(sources_1)
+    smooth(l1, 1, 7, True)
+    coarse_source(l1, l2, 2, 2, 2, True)
+
+    sources_2 = [send(s2.at[pl.ds(3, 1)], s2.at[pl.ds(1, 1)], device(1)), send(s2.at[pl.ds(2, 1)], s2.at[pl.ds(4, 1)], device(-1))]
+    smooths_1 = [send(l1.smooth.at[pl.ds(4, 1)], l1.smooth.at[pl.ds(0, 1)], device(1)), send(l1.smooth.at[pl.ds(3, 1)], l1.smooth.at[pl.ds(7, 1)], device(-1))]
     fields_3 = [
         send(db3.at[:, pl.ds(mine, 1)], db3.at[:, pl.ds(4 * (1 - dz) + across, 1)], ring_device(dz, dx)) for dz, dx in ring
     ]
-    arrive(fields_1)
-    faces(l1, 1, 7, False)
-    arrive(sources_1)
-    smooth(l1, 1, 7, False)
-    coarse_source(l1, l2, 2, 2, 2, False)
-
-    sources_2 = [send(s2.at[pl.ds(3, 1)], s2.at[pl.ds(1, 1)], device(1)), send(s2.at[pl.ds(2, 1)], s2.at[pl.ds(4, 1)], device(-1))]
-    smooths_1 = [send(l1.smooth.at[pl.ds(4, 1)], l1.smooth.at[pl.ds(0, 1)], device(1)), send(l1.smooth.at[pl.ds(3, 1)], l1.smooth.at[pl.ds(7, 1)], device(-1))]
     arrive(fields_2)
     faces(l2, 1, 5, True)
     arrive(sources_2)
@@ -408,7 +438,7 @@
     faces(l4, 1, 5, True)
     arrive(sources_3)
     smooth(l3, 1, 11, True)
-    coarse_source(l3, l4, 4, 2, 1, False)
+    coarse_source(l3, l4, 4, 2, 1, True)
     smooth(l4, 1, 5, True)
     coarse_source(l4, l5, 1, 2, 4, True)
 
@@ -450,14 +480,13 @@
     relax(l2, lifts, 1, 5, into(iterates[2]), True)
     arrive(smooths_1)
     lift(l1, iterates[2], range(1, 5), 2, 0, 8, lambda row: row // 2)
-    relax(l1, lifts, 1, 7, into(iterates[1]), False)
+    relax(l1, lifts, 1, 7, into(iterates[1]), True)
     lift(l0, iterates[1], range(1, 7), 3, 1, 11, lambda row: (row - 2) // 2 + 1)
 
     def finish(row, tile, value):
-        if 1 <= tile <= 4:
-            put(staged, row - 2, tile - 1, value)
-
-    relax(l0, lifts, 2, 10, finish, False)
+        put(staged, row - 2, tile - 1, value)
+
+    relax(l0, lifts, 2, 10, finish, False, range(1, 5))
     stores = []
     for row in range(8):
         stores.append(pltpu.make_async_copy(staged.at[row], out_ref.at[:, row, :], local_sem.at[row]))

time: 63 us -> 58.3 us (0.925)
  Pallas kernels: 60.2 us -> 55.9 us
    pallas_call x1, Pallas kernels: 60.2 us -> 55.9 us  [on_device(): pl.pallas_call(kernel, out_shape=jax.ShapeDtypeStruct((NZ, 8, 512), F32),...]
where the time goes in v3:
time: 58.3 us; the launch traced here: 57.8 us
  Pallas kernels  55.9 us (96%)
  local copies, waits for them, and re-layouts  1.87 us (3%)
    pallas_call x1, Pallas kernels, on_device(): pl.pallas_call(kernel, out_shape=jax.ShapeDtypeStruct((NZ, 8, 512), F32),...  55.9 us
    unnamed x1, local copies, waits for them, and re-layouts  1.87 us

profile of v3, /device:TPU:6, one launch (start us, length us, event | category | flops | bytes accessed | tf_op | source)
XLA Modules:
  0.0 57.8 jit_solution(4861189352294738485)
XLA Ops:
  0.0 55.9 %shard_map.37 = f32[32,8,512]{2,1,0:T(8,128)} custom-call(f32[32,8,512]{2,1,0:T(8,128)} %right_ref.1, f32[32,8,512]{2,1,0:T(8,128)} %conduct_ref.1, f32[32,8,512]{2,1,0:T(8,128)} %binding_ref.1), custom_call_target="tpu_custom_call" | custom-call | tf_op jit(solution)/shard_map/pallas_call | solution.py:515
  55.9 1.9 %copy.5 = f32[32,8,512]{2,1,0:T(8,128)} copy(f32[32,8,512]{2,1,0:T(8,128)} %shard_map.37) | data formatting | bytes 1048576

commit v4 on v3

--- a/solution.py
+++ b/solution.py
@@ -236,7 +236,7 @@
 
     inner = pl.ds(LANES, 4 * LANES)
     loads = []
-    for i, (ref, target) in enumerate(((conduct_ref, d0), (right_ref, sb0.at[0]), (binding_ref, sb0.at[1]))):
+    for i, (ref, target) in enumerate(((conduct_ref, d0), (binding_ref, sb0.at[1]), (right_ref, sb0.at[0]))):
         for row in range(8):
             loads.append(pltpu.make_async_copy(ref.at[:, row, :], target.at[2 + row, :, inner], local_sem.at[8 * i + row]))
             loads[-1].start()
@@ -269,27 +269,31 @@
         for copy in group:
             copy.wait_recv()
 
-    first = []
-    for to, near, second in ((1, 7, 6), (-1, 0, 1)):
-        halo = 1 if to == 1 else 10
-        first.append(send(conduct_ref.at[:, near, :], d0.at[halo, :, inner], device(to)))
-        first.append(send(conduct_ref.at[:, second, :], d0.at[halo - to, :, inner], device(to)))
-        first.append(send(right_ref.at[:, near, :], sb0.at[0, halo, :, inner], device(to)))
-        first.append(send(binding_ref.at[:, near, :], sb0.at[1, halo, :, inner], device(to)))
     for load in loads[:8]:
         load.wait()
-
+    rows_d = [send(d0.at[pl.ds(8, 2), :, inner], d0.at[pl.ds(0, 2), :, inner], device(1)), send(d0.at[pl.ds(2, 2), :, inner], d0.at[pl.ds(10, 2), :, inner], device(-1))]
     def sideways(source, spans):
+        sent = []
         for b in (1, -1):
             lanes_from, lanes_to = (pl.ds(4 * LANES, LANES), pl.ds(0, LANES)) if b == 1 else (pl.ds(LANES, LANES), pl.ds(5 * LANES, LANES))
             for a, rows_from, rows_to in spans:
-                first.append(send(source.at[..., rows_from, :, lanes_from], source.at[..., rows_to, :, lanes_to], device(a, b)))
-
-    sideways(d0, ((0, pl.ds(2, 8), pl.ds(2, 8)), (1, pl.ds(8, 2), pl.ds(0, 2)), (-1, pl.ds(2, 2), pl.ds(10, 2))))
-    for load in loads[8:]:
+                sent.append(send(source.at[rows_from, :, lanes_from], source.at[rows_to, :, lanes_to], device(a, b)))
+        return sent
+
+    beside = ((0, pl.ds(2, 8), pl.ds(2, 8)),)
+    corner = ((1, pl.ds(9, 1), pl.ds(1, 1)), (-1, pl.ds(2, 1), pl.ds(10, 1)))
+    lanes_d = sideways(d0, beside)
+    corners_d = sideways(d0, ((1, pl.ds(8, 2), pl.ds(0, 2)), (-1, pl.ds(2, 2), pl.ds(10, 2))))
+    for load in loads[8:16]:
         load.wait()
-    for field in (sb0.at[0], sb0.at[1]):
-        sideways(field, ((0, pl.ds(2, 8), pl.ds(2, 8)), (1, pl.ds(9, 1), pl.ds(1, 1)), (-1, pl.ds(2, 1), pl.ds(10, 1))))
+    rows_b = [send(sb0.at[1, pl.ds(9, 1), :, inner], sb0.at[1, pl.ds(1, 1), :, inner], device(1)), send(sb0.at[1, pl.ds(2, 1), :, inner], sb0.at[1, pl.ds(10, 1), :, inner], device(-1))]
+    lanes_b = sideways(sb0.at[1], beside)
+    corners_b = sideways(sb0.at[1], corner)
+    for load in loads[16:]:
+        load.wait()
+    rows_s = [send(sb0.at[0, pl.ds(9, 1), :, inner], sb0.at[0, pl.ds(1, 1), :, inner], device(1)), send(sb0.at[0, pl.ds(2, 1), :, inner], sb0.at[0, pl.ds(10, 1), :, inner], device(-1))]
+    lanes_s = sideways(sb0.at[0], beside)
+    corners_s = sideways(sb0.at[0], corner)
 
     l0, l1, l2, l3, l4, l5 = levels
     factors_0, deep_0 = l0.y_factors(), l0.z_factor()
@@ -306,7 +310,46 @@
     for_rows(2, 9, inside, False)
     face_y(l0, 9, range(1, 4), factors_0)
     face_z(l0, 9, range(1, 5), deep_0)
-    arrive(first)
+
+    arrive(rows_d)
+    for row in (0, 1, 9, 10):
+        face_x(l0, row, range(1, 5))
+    for row in (1, 10):
+        face_y(l0, row, range(1, 4), factors_0)
+        face_z(l0, row, range(1, 5), deep_0)
+    for row in (2, 9):
+        weigh(l0, row, (2, 3))
+    arrive(lanes_d)
+
+    def outside(row):
+        face_y(l0, row, (0, 4, 5), factors_0)
+        face_z(l0, row, (0, 5), deep_0)
+
+    def outside_x(row):
+        outside(row)
+        face_x(l0, row, (0, 5))
+
+    for_rows(3, 9, outside_x, False)
+    outside_x(2)
+    outside(9)
+    arrive(lanes_b)
+    for_rows(3, 9, lambda row: weigh(l0, row, (0, 1, 4, 5)), False)
+    for row in (2, 9):
+        weigh(l0, row, (1, 4))
+    arrive(rows_b)
+    for row in (1, 10):
+        weigh(l0, row, (2, 3))
+    arrive(corners_d)
+    for row in (0, 1, 9, 10):
+        face_x(l0, row, (0, 5))
+    for row in (1, 10):
+        face_y(l0, row, (0, 4, 5), factors_0)
+        face_z(l0, row, (0, 5), deep_0)
+    arrive(corners_b)
+    for row in (2, 9):
+        weigh(l0, row, (0, 5))
+    for row in (1, 10):
+        weigh(l0, row, (0, 1, 4, 5))
 
     def coarse_field(fine, coarse, n_rows, fine_row, coarse_row):
         tiles = [
@@ -357,26 +400,7 @@
         fields_1.append(send(db1.at[0, pl.ds(d_from, 1)], db1.at[0, pl.ds(d_to, 1)], device(to)))
         fields_1.append(send(db1.at[1, pl.ds(b_from, 1)], db1.at[1, pl.ds(b_to, 1)], device(to)))
 
-    def outside(row):
-        face_x(l0, row, (0, 5))
-        face_y(l0, row, (0, 4, 5), factors_0)
-        face_z(l0, row, (0, 5), deep_0)
-
-    for row in (0, 1, 9, 10):
-        face_x(l0, row, range(6))
-    for row in (1, 10):
-        face_y(l0, row, range(6), factors_0)
-        face_z(l0, row, range(6), deep_0)
-
-    def weigh_rim(row):
-        outside(row)
-        weigh(l0, row, (0, 1, 4, 5))
-
-    outside(2)
-    for_rows(3, 9, weigh_rim, False)
-    outside(9)
-    for row in (1, 2, 9, 10):
-        weigh(l0, row, range(6))
+    arrive(rows_s + lanes_s + corners_s)
     smooth(l0, 1, 11, False)
     coarse_source(l0, l1, 4, 2, 2, False)
 
@@ -483,14 +507,15 @@
     relax(l1, lifts, 1, 7, into(iterates[1]), True)
     lift(l0, iterates[1], range(1, 7), 3, 1, 11, lambda row: (row - 2) // 2 + 1)
 
+    stores = []
+
     def finish(row, tile, value):
         put(staged, row - 2, tile - 1, value)
-
-    relax(l0, lifts, 2, 10, finish, False, range(1, 5))
-    stores = []
-    for row in range(8):
-        stores.append(pltpu.make_async_copy(staged.at[row], out_ref.at[:, row, :], local_sem.at[row]))
-        stores[-1].start()
+        if tile == 4:
+            stores.append(pltpu.make_async_copy(staged.at[row - 2], out_ref.at[:, row - 2, :], local_sem.at[row - 2]))
+            stores[-1].start()
+
+    relax(l0, lifts, 2, 10, finish, True, range(1, 5))
     for copy in stores:
         copy.wait()
     for copy in copies:

time: 58.3 us -> 56 us (0.961)
  Pallas kernels: 55.9 us -> 53.8 us
    pallas_call x1, Pallas kernels: 55.9 us -> 53.8 us  [on_device(): pl.pallas_call(kernel, out_shape=jax.ShapeDtypeStruct((NZ, 8, 512), F32),...]
where the time goes in v4:
time: 56 us; the launch traced here: 55.7 us
  Pallas kernels  53.8 us (96%)
  local copies, waits for them, and re-layouts  1.87 us (3%)
    pallas_call x1, Pallas kernels, on_device(): pl.pallas_call(kernel, out_shape=jax.ShapeDtypeStruct((NZ, 8, 512), F32),...  53.8 us
    unnamed x1, local copies, waits for them, and re-layouts  1.87 us

profile of v4, /device:TPU:6, one launch (start us, length us, event | category | flops | bytes accessed | tf_op | source)
XLA Modules:
  0.0 55.7 jit_solution(14113827298950939752)
XLA Ops:
  0.0 53.8 %shard_map.37 = f32[32,8,512]{2,1,0:T(8,128)} custom-call(f32[32,8,512]{2,1,0:T(8,128)} %right_ref.1, f32[32,8,512]{2,1,0:T(8,128)} %conduct_ref.1, f32[32,8,512]{2,1,0:T(8,128)} %binding_ref.1), custom_call_target="tpu_custom_call" | custom-call | tf_op jit(solution)/shard_map/pallas_call | solution.py:540
  53.8 1.9 %copy.5 = f32[32,8,512]{2,1,0:T(8,128)} copy(f32[32,8,512]{2,1,0:T(8,128)} %shard_map.37) | data formatting | bytes 1048576

commit v5 on v4

--- a/solution.py
+++ b/solution.py
@@ -219,7 +219,7 @@
     def device(across_span, across_width=0):
         return (lax.rem(span_at + (across_span + SPAN), SPAN), lax.rem(width_at + (across_width + WIDTH), WIDTH))
 
-    ring = [(dz, dx) for dz in (0, 1, -1) for dx in range(4) if (dz, dx) != (0, 0)]
+    ring = [(1, 2), (-1, 2), (1, 1), (-1, 1), (1, 3), (-1, 3), (0, 2), (1, 0), (-1, 0), (0, 1), (0, 3)]
 
     def ring_device(dz, dx):
         to = lax.rem(across + dx, 4)
@@ -456,7 +456,7 @@
     for i in range(2):
         packed_fields[i, 4] = pack(db5[i, 4])
     fields_5 = [
-        send(packed_fields.at[:, pl.ds(4, 1)], packed_fields.at[:, pl.ds(4 - dz, 1)], device(4 * dz)) for dz in (1, -1, 2, -2, 3, -3, 4, -4)
+        send(packed_fields.at[:, pl.ds(4, 1)], packed_fields.at[:, pl.ds(4 - dz, 1)], device(4 * dz)) for dz in (4, -4, 3, -3, 2, -2, 1, -1)
     ]
     faces(l3, 1, 11, False)
     faces(l4, 1, 5, True)
@@ -467,7 +467,7 @@
     coarse_source(l4, l5, 1, 2, 4, True)
 
     packed_source[4] = pack(s5[4])
-    sources_5 = [send(packed_source.at[pl.ds(4, 1)], packed_source.at[pl.ds(4 - dz, 1)], device(4 * dz)) for dz in (1, -1, 2, -2, 3, -3)]
+    sources_5 = [send(packed_source.at[pl.ds(4, 1)], packed_source.at[pl.ds(4 - dz, 1)], device(4 * dz)) for dz in (3, -3, 2, -2, 1, -1)]
     smooths_4 = [send(l4.smooth.at[pl.ds(2, 1)], l4.smooth.at[pl.ds(0, 1)], device(4)), send(l4.smooth.at[pl.ds(3, 1)], l4.smooth.at[pl.ds(5, 1)], device(-4))]
     arrive(fields_5)
     for row in (0, 1, 2, 3, 5, 6, 7, 8):

time: 56 us -> 55.3 us (0.987)
  Pallas kernels: 53.8 us -> 52.6 us
    pallas_call x1, Pallas kernels: 53.8 us -> 52.6 us  [on_device(): pl.pallas_call(kernel, out_shape=jax.ShapeDtypeStruct((NZ, 8, 512), F32),...]
where the time goes in v5:
time: 55.3 us; the launch traced here: 54.5 us
  Pallas kernels  52.6 us (95%)
  local copies, waits for them, and re-layouts  1.87 us (3%)
    pallas_call x1, Pallas kernels, on_device(): pl.pallas_call(kernel, out_shape=jax.ShapeDtypeStruct((NZ, 8, 512), F32),...  52.6 us
    unnamed x1, local copies, waits for them, and re-layouts  1.87 us

profile of v5, /device:TPU:6, one launch (start us, length us, event | category | flops | bytes accessed | tf_op | source)
XLA Modules:
  0.0 54.5 jit_solution(18365999804751358948)
XLA Ops:
  0.0 52.6 %shard_map.37 = f32[32,8,512]{2,1,0:T(8,128)} custom-call(f32[32,8,512]{2,1,0:T(8,128)} %right_ref.1, f32[32,8,512]{2,1,0:T(8,128)} %conduct_ref.1, f32[32,8,512]{2,1,0:T(8,128)} %binding_ref.1), custom_call_target="tpu_custom_call" | custom-call | tf_op jit(solution)/shard_map/pallas_call | solution.py:540
  52.6 1.9 %copy.5 = f32[32,8,512]{2,1,0:T(8,128)} copy(f32[32,8,512]{2,1,0:T(8,128)} %shard_map.37) | data formatting | bytes 1048576

commit v6 on v5

--- a/solution.py
+++ b/solution.py
@@ -237,7 +237,7 @@
     inner = pl.ds(LANES, 4 * LANES)
     loads = []
     for i, (ref, target) in enumerate(((conduct_ref, d0), (binding_ref, sb0.at[1]), (right_ref, sb0.at[0]))):
-        for row in range(8):
+        for row in (0, 7, 1, 6, 2, 3, 4, 5):
             loads.append(pltpu.make_async_copy(ref.at[:, row, :], target.at[2 + row, :, inner], local_sem.at[8 * i + row]))
             loads[-1].start()
 
@@ -269,7 +269,7 @@
         for copy in group:
             copy.wait_recv()
 
-    for load in loads[:8]:
+    for load in loads[:4]:
         load.wait()
     rows_d = [send(d0.at[pl.ds(8, 2), :, inner], d0.at[pl.ds(0, 2), :, inner], device(1)), send(d0.at[pl.ds(2, 2), :, inner], d0.at[pl.ds(10, 2), :, inner], device(-1))]
     def sideways(source, spans):
@@ -282,6 +282,8 @@
 
     beside = ((0, pl.ds(2, 8), pl.ds(2, 8)),)
     corner = ((1, pl.ds(9, 1), pl.ds(1, 1)), (-1, pl.ds(2, 1), pl.ds(10, 1)))
+    for load in loads[4:8]:
+        load.wait()
     lanes_d = sideways(d0, beside)
     corners_d = sideways(d0, ((1, pl.ds(8, 2), pl.ds(0, 2)), (-1, pl.ds(2, 2), pl.ds(10, 2))))
     for load in loads[8:16]:
@@ -400,8 +402,15 @@
         fields_1.append(send(db1.at[0, pl.ds(d_from, 1)], db1.at[0, pl.ds(d_to, 1)], device(to)))
         fields_1.append(send(db1.at[1, pl.ds(b_from, 1)], db1.at[1, pl.ds(b_to, 1)], device(to)))
 
+    def smooth_tiles(row, tiles):
+        for tile in tiles:
+            put(l0.smooth, row, tile, tile_of(l0.weight, row, tile) * tile_of(l0.source, row, tile))
+
+    for_rows(2, 10, lambda row: smooth_tiles(row, range(1, 5)), False)
     arrive(rows_s + lanes_s + corners_s)
-    smooth(l0, 1, 11, False)
+    for_rows(2, 10, lambda row: smooth_tiles(row, (0, 5)), False)
+    for row in (1, 10):
+        smooth_tiles(row, range(6))
     coarse_source(l0, l1, 4, 2, 2, False)
 
     sources_1 = [send(s1.at[pl.ds(5, 1)], s1.at[pl.ds(1, 1)], device(1)), send(s1.at[pl.ds(2, 1)], s1.at[pl.ds(6, 1)], device(-1))]

time: 55.3 us -> 55.4 us (level)
  no operation moved by 1% of the time
where the time goes in v6:
time: 55.4 us; the launch traced here: 54.4 us
  Pallas kernels  52.5 us (95%)
  local copies, waits for them, and re-layouts  1.87 us (3%)
    pallas_call x1, Pallas kernels, on_device(): pl.pallas_call(kernel, out_shape=jax.ShapeDtypeStruct((NZ, 8, 512), F32),...  52.5 us
    unnamed x1, local copies, waits for them, and re-layouts  1.87 us

profile of v6, /device:TPU:6, one launch (start us, length us, event | category | flops | bytes accessed | tf_op | source)
XLA Modules:
  0.0 54.4 jit_solution(2985202350828290724)
XLA Ops:
  0.0 52.5 %shard_map.37 = f32[32,8,512]{2,1,0:T(8,128)} custom-call(f32[32,8,512]{2,1,0:T(8,128)} %right_ref.1, f32[32,8,512]{2,1,0:T(8,128)} %conduct_ref.1, f32[32,8,512]{2,1,0:T(8,128)} %binding_ref.1), custom_call_target="tpu_custom_call" | custom-call | tf_op jit(solution)/shard_map/pallas_call | solution.py:549
  52.5 1.9 %copy.5 = f32[32,8,512]{2,1,0:T(8,128)} copy(f32[32,8,512]{2,1,0:T(8,128)} %shard_map.37) | data formatting | bytes 1048576
